TPU v7x, 128 devices: a whole 4x4x4 slice. The times are simulated.
128 devices in a mesh: row: 8 (over z_lo, x), col: 16 (over y, z_hi, core).
Axes of the slice: x: 4, y: 4, z: 4 (z_hi: 2, z_lo: 2; z = z_hi * 2 + z_lo), core: 2. Of those that a mesh axis runs over, the one named last changes fastest.
Arguments:
- positions: float32 [3, 16384, 128], P(None, ('row', 'col')), may hold values from -6 to 6
- block_links: int32 [2, 16384], replicated, may hold values from 0 to 16383, as said below
- panel_points: int32 [8, 256], replicated, may hold values from 0 to 2097151
Outputs:
- smoothed: float32 [3, 32768, 128], P(None, ('row', 'col'))
- velocity: float32 [8, 3, 256], P('row', None, 'col')
Inputs may be any that keep to these rules, and one draw needn't show every extreme that they name: block_links[0, b] is an owner device, numbered in the order of row+col; block_links[1] is a permutation of the 16384 blocks whose cycles are the loops, and all blocks of one loop have one owner. The 128 blocks of one device, b // 128, include at most 2 of any one owner, and in every draw one owner has exactly 2 blocks on every device.
All inputs are finite; a program needn't handle non-finite values.
Results may differ from a plain program's by a relative error of at most 0.0003.
Values sent between devices are 32-bit elements; how exact they have to be, the bound alone decides.
A program may use at most 128 MiB of HBM per device.

v0:
```python
import math

import jax
import jax.numpy as jnp
from jax import lax
from jax.sharding import PartitionSpec as P

SWEEPS = 2


SMOOTH_RATE = 0.25
CORE_SQUARED = 0.01


def cross_three(left_vec, right_vec):
    return jnp.stack(
        [
            left_vec[1] * right_vec[2] - left_vec[2] * right_vec[1],
            left_vec[2] * right_vec[0] - left_vec[0] * right_vec[2],
            left_vec[0] * right_vec[1] - left_vec[1] * right_vec[0],
        ]
    )


def neighbours(points, next_slot, prev_slot):
    ahead = jnp.concatenate([points[:, :, 1:], points[:, next_slot, :1]], axis=2)
    behind = jnp.concatenate([points[:, prev_slot, -1:], points[:, :, :-1]], axis=2)
    return (behind, ahead)


def smooth_loops(points, next_slot, prev_slot):
    for sweep_no in range(SWEEPS):
        behind, ahead = neighbours(points, next_slot, prev_slot)
        points = points + SMOOTH_RATE * (behind - 2.0 * points + ahead)
    return points


def panel_sums(targets, sources):
    centres = sources[:3]
    segments = sources[3:]
    inner = lax.dot_general(
        targets, centres, (((0,), (0,)), ((), ())), precision=lax.Precision.HIGHEST
    )
    squared = (
        jnp.sum(targets * targets, 0)[:, None]
        + jnp.sum(centres * centres, 0)[None, :]
        - 2.0 * inner
        + CORE_SQUARED
    )
    weights = 1.0 / (squared * jnp.sqrt(squared))
    features = jnp.concatenate([segments, cross_three(segments, centres)], 0)
    return lax.dot_general(
        weights, features, (((1,), (1,)), ((), ())), precision=lax.Precision.HIGHEST
    )


def tiled_sums(targets, piece, running, largest):
    blocks = piece.shape[1]
    block_len = piece.shape[2]
    group = max(
        [
            size_try
            for size_try in (1, 2, 4, 8, 16, 32, 64, 128)
            if blocks % size_try == 0 and size_try <= largest
        ]
    )

    def one_tile(turn, accum):
        tile = lax.dynamic_slice_in_dim(piece, turn * group, group, 1).reshape(6, group * block_len)
        return accum + panel_sums(targets, tile)

    return lax.fori_loop(0, blocks // group, one_tile, running)


def shards(positions, block_links, panel_points):
    devices = lax.axis_size(("row", "col"))
    my_index = lax.axis_index(("row", "col"))
    slots = positions.shape[1]
    block_len = positions.shape[2]
    capacity = 2 * slots // devices
    held_slots = devices * capacity
    owners = block_links[0]
    follows = block_links[1]
    blocks_all = owners.shape[0]
    counter = jnp.arange(blocks_all, dtype=jnp.int32)
    precedes = jnp.zeros_like(follows).at[follows].set(counter)
    owner_grid = owners.reshape(devices, slots)
    same_owner = owner_grid[:, :, None] == owner_grid[:, None, :]
    earlier = jnp.arange(slots)[None, :] < jnp.arange(slots)[:, None]
    ranks = jnp.sum(jnp.logical_and(same_owner, earlier[None]), axis=2).reshape(blocks_all)
    places = counter // slots * capacity + ranks
    my_owner = lax.dynamic_slice_in_dim(owners, my_index * slots, slots)
    my_rank = lax.dynamic_slice_in_dim(ranks, my_index * slots, slots)
    outgoing_slot = my_owner * capacity + my_rank
    outgoing = (
        jnp.zeros((3, held_slots, block_len), jnp.float32).at[:, outgoing_slot, :].set(positions)
    )
    arrived = lax.all_to_all(outgoing, ("row", "col"), split_axis=1, concat_axis=1, tiled=True)
    is_owned = owners == my_index
    held_ids = (
        jnp.full((held_slots,), blocks_all, jnp.int32)
        .at[jnp.where(is_owned, places, held_slots)]
        .set(counter, mode="drop")
    )
    live = held_ids < blocks_all
    safe_ids = jnp.minimum(held_ids, blocks_all - 1)
    slot_index = jnp.arange(held_slots, dtype=jnp.int32)
    next_slot = jnp.where(live, places[follows[safe_ids]], slot_index)
    prev_slot = jnp.where(live, places[precedes[safe_ids]], slot_index)
    smoothed = smooth_loops(arrived, next_slot, prev_slot)
    behind, ahead = neighbours(smoothed, next_slot, prev_slot)
    segments = ahead - smoothed
    centres = 0.5 * (ahead + smoothed)
    sources = jnp.concatenate([centres, segments], 0)
    wanted = panel_points.reshape(-1)
    wanted_block = wanted // block_len
    wanted_point = wanted % block_len
    wanted_mine = owners[wanted_block] == my_index
    picked = smoothed[:, places[wanted_block], wanted_point]
    local_targets = jnp.where(wanted_mine[None, :], picked, 0.0)
    all_targets = lax.psum(local_targets, ("row", "col"))
    panel = panel_points.shape[1]
    col_count = lax.axis_size("col")
    share = panel // col_count
    scale = 1.0 / (math.pi * math.sqrt(blocks_all * block_len))
    targets = lax.dynamic_slice_in_dim(all_targets, lax.axis_index("row") * panel, panel, 1)
    zero_sums = jnp.zeros((panel, 6), jnp.float32)
    sums = tiled_sums(targets, lax.all_gather(sources, "row", axis=1, tiled=True), zero_sums, 128)
    partial_velocity = scale * (cross_three(sums[:, :3].T, targets) - sums[:, 3:].T)
    summed = lax.psum(partial_velocity, "col")
    velocity_part = lax.dynamic_slice_in_dim(summed, lax.axis_index("col") * share, share, 1)
    return (smoothed, velocity_part[None])


def solution(mesh):
    placed = (P(None, ("row", "col"), None), P(), P())
    return jax.shard_map(
        shards,
        mesh=mesh,
        in_specs=placed,
        out_specs=(P(None, ("row", "col"), None), P("row", None, "col")),
        check_vma=False,
    )
```

profile of v0, /device:TPU:1, one launch (start us, length us, event | category | flops | bytes accessed | tf_op | source)
XLA Modules:
  0.0 973.3 jit_solution(4487103491891929501)
XLA Ops:
  15.4 12.4 %scatter_fusion = f32[3,256,128]{2,0,1:T(4,128)} fusion(f32[3,256,128]{2,0,1:T(4,128)} %broadcast_in_dim.36, s32[128]{0:T(128)S(1)} %compare_select_fusion.13, f32[128,3,128]{2,1,0:T(4,128)S(1)} %copy.77), kind=kCustom, calls=%fused_computation.12 | custom fusion | bytes 590336 | tf_op jit(solution)/shard_map/scatter | solution.py:96
  27.9 11.6 %all-to-all-start = ((f32[3,256,128]{2,0,1:T(4,128)}), f32[3,256,128]{2,0,1:T(4,128)S(1)}, u32[]{:S(2)}, u32[]{:S(2)}) async-start(f32[3,256,128]{2,0,1:T(4,128)} %scatter_fusion), calls=%async_computation | async-start | bytes 1048576 | tf_op jit(solution)/shard_map/all_to_all | solution.py:98
  40.7 60.3 %scatter_custom_fusion.1 = s32[256]{0:T(256)S(1)} fusion(s32[16384]{0:T(1024)S(1)} %bitcast.119, s32[16384]{0:T(1024)S(1)} %iota.31, s32[]{:T(128)} %constant.150.clone.1), kind=kCustom, calls=%fused_computation.120 | custom fusion | bytes 1028 | tf_op jit(solution)/shard_map/scatter | solution.py:103
  101.1 60.5 %scatter_custom_fusion.2 = s32[16384]{0:T(1024)S(1)} fusion(s32[16384]{0:T(1024)S(1)} %bitcast.118, s32[16384]{0:T(1024)S(1)} %iota.33, s32[]{:T(128)} %constant.144.clone.1), kind=kCustom, calls=%fused_computation.79 | custom fusion | bytes 65540 | tf_op jit(solution)/shard_map/scatter | solution.py:86
  218.2 11.8 %gather_fusion.9 = s32[2048]{0:T(1024)S(1)} fusion(s32[16384]{0:T(1024)S(1)} %fusion.28, s32[2048]{0:T(1024)S(1)} %broadcast_clamp_fusion), kind=kCustom, calls=%fused_computation.9 | custom fusion | bytes 24576 | tf_op jit(solution)/shard_map/gather | solution.py:119
  230.0 11.8 %gather_fusion.8 = s32[2048]{0:T(1024)S(1)} fusion(s32[16384]{0:T(1024)S(1)} %bitcast.99, s32[2048]{0:T(1024)S(1)} %broadcast_clamp_fusion), kind=kCustom, calls=%fused_computation.8 | custom fusion | bytes 24576 | tf_op jit(solution)/shard_map/gather | solution.py:118
  242.6 20.8 %gather_fusion.10 = f32[2048,3]{1,0:T(8,128)S(1)} fusion(f32[3,256,128]{0,2,1:T(8,128)} %copy.90, s32[2048]{0:T(1024)S(1)} %bitcast.100), kind=kCustom, calls=%fused_computation.10 | custom fusion | bytes 65536 | tf_op jit(solution)/shard_map/gather | solution.py:119
  263.8 81.0 %psum.14 = f32[3,2048]{0,1:T(8,128)S(1)} all-reduce(f32[3,2048]{0,1:T(8,128)S(1)} %select_bitcast_fusion), channel_id=1, replica_groups=mesh['row'=8,'col'=16] {'row','col'}, use_global_device_ids=true, to_apply=%region_4.5 | all-reduce | flops 6144 | bytes 49152 | tf_op jit(solution)/shard_map/psum | solution.py:121
  345.5 586.7 %while.16 = (s32[]{:T(128)}, f32[256,6]{0,1:T(8,128)S(1)}, f32[256]{0:T(256)S(1)}, f32[6,2048,128]{2,1,0:T(8,128)}, f32[3,256]{1,0:T(4,128)S(1)}, /*index=5*/s32...) while((s32[]{:T(128)}, f32[256,6]{0,1:T(8,128)S(1)}, ...), condition=%wide.region_8.9_spmd.clone, body=%wide.region_6.8_spmd.clone.sunk | while | flops 478678016 | bytes 36061472 | solution.py:72
  347.9 25.7 %sqrt_multiply_fusion.2 = f32[256,16384]{0,1:T(8,128)S(1)} fusion(f32[3,256]{1,0:T(4,128)S(1)} %get-tuple-element.277, f32[16384]{0:T(1024)S(1)} %bitcast.107, f32[256]{0:T(256)S(1)} %get-tuple-element.275, f32[1,3,128,128]{3,2,1,0:T(8,128)S(1)} %get-tuple-element.240), kind=kOutput, calls=%fused_computation.15.clone.1 | convolution fusion | flops 171966464 | bytes 17043456 | tf_op jit(solution)/shard_map/while/body/eval_jaxpr/dot_general | solution.py:41
  373.6 8.8 fusion.67
  384.6 25.7 %sqrt_multiply_fusion.2 = f32[256,16384]{0,1:T(8,128)S(1)} fusion(f32[3,256]{1,0:T(4,128)S(1)} %get-tuple-element.277, f32[16384]{0:T(1024)S(1)} %bitcast.107, f32[256]{0:T(256)S(1)} %get-tuple-element.275, f32[1,3,128,128]{3,2,1,0:T(8,128)S(1)} %get-tuple-element.240), kind=kOutput, calls=%fused_computation.15.clone.1 | convolution fusion | flops 171966464 | bytes 17043456 | tf_op jit(solution)/shard_map/while/body/eval_jaxpr/dot_general | solution.py:41
  410.2 8.8 fusion.67
  421.2 25.7 %sqrt_multiply_fusion.2 = f32[256,16384]{0,1:T(8,128)S(1)} fusion(f32[3,256]{1,0:T(4,128)S(1)} %get-tuple-element.277, f32[16384]{0:T(1024)S(1)} %bitcast.107, f32[256]{0:T(256)S(1)} %get-tuple-element.275, f32[1,3,128,128]{3,2,1,0:T(8,128)S(1)} %get-tuple-element.240), kind=kOutput, calls=%fused_computation.15.clone.1 | convolution fusion | flops 171966464 | bytes 17043456 | tf_op jit(solution)/shard_map/while/body/eval_jaxpr/dot_general | solution.py:41
  446.9 8.8 fusion.67
  457.9 25.7 %sqrt_multiply_fusion.2 = f32[256,16384]{0,1:T(8,128)S(1)} fusion(f32[3,256]{1,0:T(4,128)S(1)} %get-tuple-element.277, f32[16384]{0:T(1024)S(1)} %bitcast.107, f32[256]{0:T(256)S(1)} %get-tuple-element.275, f32[1,3,128,128]{3,2,1,0:T(8,128)S(1)} %get-tuple-element.240), kind=kOutput, calls=%fused_computation.15.clone.1 | convolution fusion | flops 171966464 | bytes 17043456 | tf_op jit(solution)/shard_map/while/body/eval_jaxpr/dot_general | solution.py:41
  483.6 8.8 fusion.67
  494.6 25.7 %sqrt_multiply_fusion.2 = f32[256,16384]{0,1:T(8,128)S(1)} fusion(f32[3,256]{1,0:T(4,128)S(1)} %get-tuple-element.277, f32[16384]{0:T(1024)S(1)} %bitcast.107, f32[256]{0:T(256)S(1)} %get-tuple-element.275, f32[1,3,128,128]{3,2,1,0:T(8,128)S(1)} %get-tuple-element.240), kind=kOutput, calls=%fused_computation.15.clone.1 | convolution fusion | flops 171966464 | bytes 17043456 | tf_op jit(solution)/shard_map/while/body/eval_jaxpr/dot_general | solution.py:41
  520.2 8.8 fusion.67
  531.2 25.7 %sqrt_multiply_fusion.2 = f32[256,16384]{0,1:T(8,128)S(1)} fusion(f32[3,256]{1,0:T(4,128)S(1)} %get-tuple-element.277, f32[16384]{0:T(1024)S(1)} %bitcast.107, f32[256]{0:T(256)S(1)} %get-tuple-element.275, f32[1,3,128,128]{3,2,1,0:T(8,128)S(1)} %get-tuple-element.240), kind=kOutput, calls=%fused_computation.15.clone.1 | convolution fusion | flops 171966464 | bytes 17043456 | tf_op jit(solution)/shard_map/while/body/eval_jaxpr/dot_general | solution.py:41
  556.9 8.8 fusion.67
  567.9 25.7 %sqrt_multiply_fusion.2 = f32[256,16384]{0,1:T(8,128)S(1)} fusion(f32[3,256]{1,0:T(4,128)S(1)} %get-tuple-element.277, f32[16384]{0:T(1024)S(1)} %bitcast.107, f32[256]{0:T(256)S(1)} %get-tuple-element.275, f32[1,3,128,128]{3,2,1,0:T(8,128)S(1)} %get-tuple-element.240), kind=kOutput, calls=%fused_computation.15.clone.1 | convolution fusion | flops 171966464 | bytes 17043456 | tf_op jit(solution)/shard_map/while/body/eval_jaxpr/dot_general | solution.py:41
  604.5 25.7 %sqrt_multiply_fusion.2 = f32[256,16384]{0,1:T(8,128)S(1)} fusion(f32[3,256]{1,0:T(4,128)S(1)} %get-tuple-element.277, f32[16384]{0:T(1024)S(1)} %bitcast.107, f32[256]{0:T(256)S(1)} %get-tuple-element.275, f32[1,3,128,128]{3,2,1,0:T(8,128)S(1)} %get-tuple-element.240), kind=kOutput, calls=%fused_computation.15.clone.1 | convolution fusion | flops 171966464 | bytes 17043456 | tf_op jit(solution)/shard_map/while/body/eval_jaxpr/dot_general | solution.py:41
  641.2 25.7 %sqrt_multiply_fusion.2 = f32[256,16384]{0,1:T(8,128)S(1)} fusion(f32[3,256]{1,0:T(4,128)S(1)} %get-tuple-element.277, f32[16384]{0:T(1024)S(1)} %bitcast.107, f32[256]{0:T(256)S(1)} %get-tuple-element.275, f32[1,3,128,128]{3,2,1,0:T(8,128)S(1)} %get-tuple-element.240), kind=kOutput, calls=%fused_computation.15.clone.1 | convolution fusion | flops 171966464 | bytes 17043456 | tf_op jit(solution)/shard_map/while/body/eval_jaxpr/dot_general | solution.py:41
  677.9 25.7 %sqrt_multiply_fusion.2 = f32[256,16384]{0,1:T(8,128)S(1)} fusion(f32[3,256]{1,0:T(4,128)S(1)} %get-tuple-element.277, f32[16384]{0:T(1024)S(1)} %bitcast.107, f32[256]{0:T(256)S(1)} %get-tuple-element.275, f32[1,3,128,128]{3,2,1,0:T(8,128)S(1)} %get-tuple-element.240), kind=kOutput, calls=%fused_computation.15.clone.1 | convolution fusion | flops 171966464 | bytes 17043456 | tf_op jit(solution)/shard_map/while/body/eval_jaxpr/dot_general | solution.py:41
  714.5 25.7 %sqrt_multiply_fusion.2 = f32[256,16384]{0,1:T(8,128)S(1)} fusion(f32[3,256]{1,0:T(4,128)S(1)} %get-tuple-element.277, f32[16384]{0:T(1024)S(1)} %bitcast.107, f32[256]{0:T(256)S(1)} %get-tuple-element.275, f32[1,3,128,128]{3,2,1,0:T(8,128)S(1)} %get-tuple-element.240), kind=kOutput, calls=%fused_computation.15.clone.1 | convolution fusion | flops 171966464 | bytes 17043456 | tf_op jit(solution)/shard_map/while/body/eval_jaxpr/dot_general | solution.py:41
  751.2 25.7 %sqrt_multiply_fusion.2 = f32[256,16384]{0,1:T(8,128)S(1)} fusion(f32[3,256]{1,0:T(4,128)S(1)} %get-tuple-element.277, f32[16384]{0:T(1024)S(1)} %bitcast.107, f32[256]{0:T(256)S(1)} %get-tuple-element.275, f32[1,3,128,128]{3,2,1,0:T(8,128)S(1)} %get-tuple-element.240), kind=kOutput, calls=%fused_computation.15.clone.1 | convolution fusion | flops 171966464 | bytes 17043456 | tf_op jit(solution)/shard_map/while/body/eval_jaxpr/dot_general | solution.py:41
  787.8 25.7 %sqrt_multiply_fusion.2 = f32[256,16384]{0,1:T(8,128)S(1)} fusion(f32[3,256]{1,0:T(4,128)S(1)} %get-tuple-element.277, f32[16384]{0:T(1024)S(1)} %bitcast.107, f32[256]{0:T(256)S(1)} %get-tuple-element.275, f32[1,3,128,128]{3,2,1,0:T(8,128)S(1)} %get-tuple-element.240), kind=kOutput, calls=%fused_computation.15.clone.1 | convolution fusion | flops 171966464 | bytes 17043456 | tf_op jit(solution)/shard_map/while/body/eval_jaxpr/dot_general | solution.py:41
  824.5 25.7 %sqrt_multiply_fusion.2 = f32[256,16384]{0,1:T(8,128)S(1)} fusion(f32[3,256]{1,0:T(4,128)S(1)} %get-tuple-element.277, f32[16384]{0:T(1024)S(1)} %bitcast.107, f32[256]{0:T(256)S(1)} %get-tuple-element.275, f32[1,3,128,128]{3,2,1,0:T(8,128)S(1)} %get-tuple-element.240), kind=kOutput, calls=%fused_computation.15.clone.1 | convolution fusion | flops 171966464 | bytes 17043456 | tf_op jit(solution)/shard_map/while/body/eval_jaxpr/dot_general | solution.py:41
  861.1 25.7 %sqrt_multiply_fusion.2 = f32[256,16384]{0,1:T(8,128)S(1)} fusion(f32[3,256]{1,0:T(4,128)S(1)} %get-tuple-element.277, f32[16384]{0:T(1024)S(1)} %bitcast.107, f32[256]{0:T(256)S(1)} %get-tuple-element.275, f32[1,3,128,128]{3,2,1,0:T(8,128)S(1)} %get-tuple-element.240), kind=kOutput, calls=%fused_computation.15.clone.1 | convolution fusion | flops 171966464 | bytes 17043456 | tf_op jit(solution)/shard_map/while/body/eval_jaxpr/dot_general | solution.py:41
  897.8 25.7 %sqrt_multiply_fusion.2 = f32[256,16384]{0,1:T(8,128)S(1)} fusion(f32[3,256]{1,0:T(4,128)S(1)} %get-tuple-element.277, f32[16384]{0:T(1024)S(1)} %bitcast.107, f32[256]{0:T(256)S(1)} %get-tuple-element.275, f32[1,3,128,128]{3,2,1,0:T(8,128)S(1)} %get-tuple-element.240), kind=kOutput, calls=%fused_computation.15.clone.1 | convolution fusion | flops 171966464 | bytes 17043456 | tf_op jit(solution)/shard_map/while/body/eval_jaxpr/dot_general | solution.py:41
  932.8 32.8 %psum.15 = f32[3,256]{1,0:T(4,128)S(1)} all-reduce(f32[3,256]{1,0:T(4,128)S(1)} %fusion.41), channel_id=1, replica_groups=mesh['row'=8,'col'=16] {'col'}, use_global_device_ids=true, to_apply=%region_9.10 | all-reduce | flops 768 | bytes 6144 | tf_op jit(solution)/shard_map/psum | solution.py:130
  (129 shorter events, 192.1 us)
Async XLA Ops:
  27.9 140.7 %all-to-all-start = ((f32[3,256,128]{2,0,1:T(4,128)}), f32[3,256,128]{2,0,1:T(4,128)S(1)}, u32[]{:S(2)}, u32[]{:S(2)}) async-start(f32[3,256,128]{2,0,1:T(4,128)} %scatter_fusion), calls=%async_computation | async-start | bytes 1048576 | tf_op jit(solution)/shard_map/all_to_all | solution.py:98
  39.4 306.1 %all-gather.2.cloned.1.call-start = ((), (), s32[]{:S(2)}) async-start(), calls=%async_computation.1 | async-start | bytes 7077888 | tf_op jit(solution)/shard_map/all_gather | solution.py:128
  194.6 23.5 %copy-start = (s32[8,256]{1,0:T(8,128)S(1)}, s32[8,256]{1,0:T(8,128)}, u32[]{:S(2)}) copy-start(s32[8,256]{1,0:T(8,128)} %param.7) | copy-start | bytes 24580
Sparse Core Ops, SparseCore 0:
  218.2 75.7 all-gather.1
where the time goes:
time: 982 us; the launch traced here: 973 us
  matrix products  550 us (56%)
  local copies, waits for them, and re-layouts  239 us (24%)
  blocking collectives  114 us (12%)
  other arithmetic  42.8 us (4%)
  between operations  14.6 us (1%)
  starting transfers between devices  11.6 us (1%)
    dot_general x16, matrix products, panel_sums(): lax.dot_general(targets, centres, (((0,), (0,)), ((), ())), precision=lax...  410 us
    dot_general x16, matrix products, panel_sums(): lax.dot_general(weights, features, (((1,), (1,)), ((), ())), precision=la...  140 us
    psum x1, blocking collectives, shards(): all_targets = lax.psum(local_targets, ('row', 'col'))  81 us
    scatter x1, local copies, waits for them, and re-layouts, shards(): precedes = jnp.zeros_like(follows).at[follows].set(counter)  60.5 us
    scatter x1, local copies, waits for them, and re-layouts, shards(): held_ids = jnp.full((held_slots,), blocks_all, jnp.int32).at[jnp.where(is...  60.3 us
    psum x1, blocking collectives, shards(): summed = lax.psum(partial_velocity, 'col')  32.8 us
    gather x2, local copies, waits for them, and re-layouts, shards(): picked = smoothed[:, places[wanted_block], wanted_point]  32.6 us
  transfers between devices with their start and end apart: 2, of which 0 were waited for; matrix products, arithmetic and copies ran while one was open for 18% of the time, Pallas kernels for 0%

commit v1 on v0

v1 whole, which is shorter than its diff:
```python
import functools
import math

import jax
import jax.numpy as jnp
from jax import lax
from jax.experimental import pallas as pl
from jax.experimental.pallas import tpu as pltpu
from jax.sharding import PartitionSpec as P

CORE_SQUARED = 0.01
F32 = jnp.float32
BF16 = jnp.bfloat16
LANES = 128
VMEM_LIMIT = 56 << 20
MESH = pl.DeviceIdType.MESH
CHUNK = 6
EDGE_LANES = (125, 126, 127, 0, 1)


def iota(shape, axis):
    return lax.broadcasted_iota(jnp.int32, shape, axis)


def three_parts(value):
    high = value.astype(BF16)
    rest = value - high.astype(F32)
    middle = rest.astype(BF16)
    return high, middle, (rest - middle.astype(F32)).astype(BF16)


def two_parts(value):
    high = value.astype(BF16)
    return high, (value - high.astype(F32)).astype(BF16)


def to_column(row, eye):
    return jnp.sum(jnp.where(eye, row, 0.0), axis=1, keepdims=True)


def to_row(column, eye):
    return jnp.sum(jnp.where(eye, column, 0.0), axis=0, keepdims=True)


def pick_rows(chooser, arrays):
    width = arrays[0].shape[1]
    parts = jnp.concatenate([part for array in arrays for part in three_parts(array)], axis=1)
    got = jnp.dot(chooser, parts, preferred_element_type=F32)
    result = []
    for n in range(len(arrays)):
        at = 3 * n * width
        result.append(
            got[:, at : at + width]
            + got[:, at + width : at + 2 * width]
            + got[:, at + 2 * width : at + 3 * width]
        )
    return result


def roll(value, shift):
    return pltpu.roll(value, shift % LANES, 1)


def prep_kernel(me_ref, pos_ref, links_ref, panel_ref, out_ref, tgt_ref):
    slots = pos_ref.shape[1]
    me = me_ref[0]
    base = me * slots
    eye = iota((slots, LANES), 0) == iota((slots, LANES), 1)
    here = pl.ds(pl.multiple_of(base, LANES), LANES)
    owner_row = links_ref[0:1, here].astype(F32)
    follow_row = links_ref[1:2, here].astype(F32)
    owner_col = to_column(owner_row, eye)
    follow_col = to_column(follow_row, eye)
    earlier = iota((slots, LANES), 0) < iota((slots, LANES), 1)
    same = jnp.logical_and(owner_col == owner_row, earlier)
    rank_row = jnp.sum(jnp.where(same, 1.0, 0.0), axis=0, keepdims=True)
    slot_row = owner_row * 2.0 + rank_row
    held = out_ref.shape[1]
    chooser = (iota((held, LANES), 0).astype(F32) == slot_row).astype(BF16)
    raw = [pos_ref[c] for c in range(3)]
    for c, moved in enumerate(pick_rows(chooser, raw)):
        out_ref[c] = moved

    mine_col = (base + iota((slots, 1), 0)).astype(F32)
    blocks = links_ref.shape[1]
    lane_row = iota((1, LANES), 1).astype(F32)

    def look(turn, total):
        at = pl.multiple_of(turn * LANES, LANES)
        row = links_ref[1:2, pl.ds(at, LANES)].astype(F32)
        number = lane_row + (turn * LANES).astype(F32)
        return total + jnp.where(row == mine_col, number, 0.0)

    precede_col = jnp.sum(
        lax.fori_loop(0, blocks // LANES, look, jnp.zeros((slots, LANES), F32), unroll=8),
        axis=1,
        keepdims=True,
    )

    lane = iota((slots, LANES), 1)
    rows = []
    for c in range(3):
        x = raw[c]
        b1, b2, a1, a2 = roll(x, 1), roll(x, 2), roll(x, -1), roll(x, -2)
        zero = jnp.zeros_like(x)
        wrap = (
            4.0 * (jnp.where(lane < 1, b1, zero) + jnp.where(lane > LANES - 2, a1, zero))
            + (jnp.where(lane < 2, b2, zero) + jnp.where(lane > LANES - 3, a2, zero))
        )
        inside = (
            6.0 * x
            + 4.0 * (jnp.where(lane < 1, zero, b1) + jnp.where(lane > LANES - 2, zero, a1))
            + (jnp.where(lane < 2, zero, b2) + jnp.where(lane > LANES - 3, zero, a2))
        )
        rows += [inside * 0.0625, wrap * 0.0625]
    stack = jnp.concatenate(rows, axis=0)
    parts = jnp.concatenate(three_parts(stack), axis=0)
    high = stack.shape[0]
    width = panel_ref.shape[1]
    per_half = tgt_ref.shape[1] // width
    tgt_ref[...] = jnp.zeros_like(tgt_ref)
    for r in range(panel_ref.shape[0]):
        flat = panel_ref[r : r + 1, :]
        block = (flat // LANES).astype(F32)
        point = flat % LANES
        one_point = (iota((LANES, width), 0) == point).astype(BF16)
        got = jnp.dot(parts, one_point, preferred_element_type=F32)
        got = got[:high] + got[high : 2 * high] + got[2 * high :]
        here_mask = block == mine_col
        edge_mask = jnp.logical_or(
            jnp.logical_and(precede_col == block, point >= LANES - 2),
            jnp.logical_and(follow_col == block, point <= 1),
        )
        for c in range(3):
            at = 2 * c * slots
            value = jnp.where(here_mask, got[at : at + slots], 0.0) + jnp.where(
                edge_mask, got[at + slots : at + 2 * slots], 0.0
            )
            row = (r // per_half) * 3 + c
            col = (r % per_half) * width
            tgt_ref[row : row + 1, col : col + width] = jnp.sum(value, axis=0, keepdims=True)


def exchange_kernel(
    n_row, n_col, out_ref, part_ref, arrived_ref, tgt_ref,
    row_in, total, col_in, send_sem, recv_sem, own_sem,
    s1, r1, s2, r2, s3, r3,
):
    me_r = lax.axis_index("row")
    me_c = lax.axis_index("col")
    me = me_r * n_col + me_c
    n = n_row * n_col
    width = total.shape[1]

    def slice_of(ref, r):
        return ref.at[:, pl.ds(pl.multiple_of(r * width, width), width)]

    first = []
    for step in range(1, n_row):
        to = lax.rem(me_r + step, n_row)
        copy = pltpu.make_async_remote_copy(
            src_ref=slice_of(part_ref, to),
            dst_ref=row_in.at[me_r],
            send_sem=s1.at[step],
            recv_sem=r1.at[me_r],
            device_id=(to, me_c),
            device_id_type=MESH,
        )
        copy.start()
        first.append(copy)

    def start_block(step, carry):
        to = lax.rem(me + step, n)
        pltpu.make_async_remote_copy(
            src_ref=out_ref.at[:, to],
            dst_ref=arrived_ref.at[:, me],
            send_sem=send_sem,
            recv_sem=recv_sem,
            device_id=(to // n_col, lax.rem(to, n_col)),
            device_id_type=MESH,
        ).start()
        return carry

    lax.fori_loop(1, n, start_block, 0)
    own = pltpu.make_async_copy(out_ref.at[:, me], arrived_ref.at[:, me], own_sem)
    own.start()

    row_in[me_r] = part_ref[:, pl.ds(pl.multiple_of(me_r * width, width), width)]
    for step in range(1, n_row):
        frm = lax.rem(me_r + step, n_row)
        pltpu.make_async_copy(row_in.at[frm], row_in.at[frm], r1.at[frm]).wait()
    value = row_in[0]
    for r in range(1, n_row):
        value = value + row_in[r]
    total[...] = value
    second = []
    for step in range(1, n_col):
        to = lax.rem(me_c + step, n_col)
        copy = pltpu.make_async_remote_copy(
            src_ref=total,
            dst_ref=col_in.at[me_c],
            send_sem=s2.at[step],
            recv_sem=r2.at[me_c],
            device_id=(me_r, to),
            device_id_type=MESH,
        )
        copy.start()
        second.append(copy)
    col_in[me_c] = value
    for step in range(1, n_col):
        frm = lax.rem(me_c + step, n_col)
        pltpu.make_async_copy(col_in.at[frm], col_in.at[frm], r2.at[frm]).wait()
    value = col_in[0]
    for c in range(1, n_col):
        value = value + col_in[c]
    tgt_ref[:, pl.ds(pl.multiple_of(me_r * width, width), width)] = value
    third = []
    for step in range(1, n_row):
        to = lax.rem(me_r + step, n_row)
        copy = pltpu.make_async_remote_copy(
            src_ref=slice_of(tgt_ref, me_r),
            dst_ref=slice_of(tgt_ref, me_r),
            send_sem=s3.at[step],
            recv_sem=r3.at[me_r],
            device_id=(to, me_c),
            device_id_type=MESH,
        )
        copy.start()
        third.append(copy)
    for step in range(1, n_row):
        frm = lax.rem(me_r + step, n_row)
        pltpu.make_async_copy(slice_of(tgt_ref, frm), slice_of(tgt_ref, frm), r3.at[frm]).wait()
    for copy in first + second + third:
        copy.wait_send()
    rest = pl.ds(0, n - 1)
    pltpu.make_async_copy(out_ref.at[:, rest], out_ref.at[:, rest], send_sem).wait()
    pltpu.make_async_copy(arrived_ref.at[:, rest], arrived_ref.at[:, rest], recv_sem).wait()
    own.wait()


def features(centres, segments):
    rows = []
    for c in centres:
        high, middle, low = (part.astype(F32) for part in three_parts(c))
        rows += [high, middle, high, low, high, middle]
    square = centres[0] * centres[0] + centres[1] * centres[1] + centres[2] * centres[2]
    rows += [part.astype(F32) for part in three_parts(square)]
    rows += [jnp.ones_like(square)] * 3
    s, c = segments, centres
    six = [s[0], s[1], s[2]]
    six += [s[1] * c[2] - s[2] * c[1], s[2] * c[0] - s[0] * c[2], s[0] * c[1] - s[1] * c[0]]
    pairs = [two_parts(value) for value in six]
    return rows, [pair[0].astype(F32) for pair in pairs], [pair[1].astype(F32) for pair in pairs]


def velocity_kernel(
    scale, me_ref, pos_ref, arrived_ref, grid_ref, tgt_ref, smooth_ref, vel_ref,
    b_ref, f_ref, a_ref, acc_ref,
):
    slots = pos_ref.shape[1]
    held = arrived_ref.shape[1]
    me = me_ref[0].astype(F32)
    b_ref[...] = jnp.zeros_like(b_ref)
    f_ref[...] = jnp.zeros_like(f_ref)
    a_ref[...] = jnp.zeros_like(a_ref)

    half = tgt_ref.shape[1]
    for h in range(2):
        at = slice(h * half, (h + 1) * half)
        t = [tgt_ref[h * 3 + c : h * 3 + c + 1, :] for c in range(3)]
        rows = []
        for value in t:
            high, middle, low = (part.astype(F32) for part in three_parts(-2.0 * value))
            rows += [high, high, middle, high, low, middle]
        rows += [jnp.ones_like(t[0])] * 3
        square = t[0] * t[0] + t[1] * t[1] + t[2] * t[2] + CORE_SQUARED
        rows += [part.astype(F32) for part in three_parts(square)]
        for k, row in enumerate(rows):
            a_ref[k : k + 1, at] = row

    lane = iota((slots, LANES), 1)
    inner = jnp.logical_and(lane >= 2, lane < LANES - 3)
    centres, segments = [], []
    for c in range(3):
        x = pos_ref[c]
        sm = (6.0 * x + 4.0 * (roll(x, 1) + roll(x, -1)) + (roll(x, 2) + roll(x, -2))) * 0.0625
        ahead = roll(sm, -1)
        segments.append(jnp.where(inner, ahead - sm, 0.0))
        centres.append(0.5 * (ahead + sm))
    rows, highs, lows = features(centres, segments)
    for k, row in enumerate(rows):
        b_ref[pl.ds(k, slots, stride=32), :] = row
    for k in range(6):
        f_ref[pl.ds(k, slots, stride=16), :] = highs[k]
        f_ref[pl.ds(8 + k, slots, stride=16), :] = lows[k]

    n = grid_ref.shape[1]
    owners = grid_ref[0].astype(F32)
    follows = grid_ref[1].astype(F32)
    square_eye = iota((n, LANES), 0) == iota((n, LANES), 1)
    number = (iota((n, LANES), 0) * LANES + iota((n, LANES), 1)).astype(F32)
    mine = owners == me
    before = (iota((LANES, LANES), 0) < iota((LANES, LANES), 1)).astype(BF16)
    rank = jnp.dot(mine.astype(BF16), before, preferred_element_type=F32)
    id_col = jnp.zeros((held, 1), F32)
    next_col = jnp.zeros((held, 1), F32)
    for k in range(2):
        chosen = jnp.logical_and(mine, rank == float(k))
        count = jnp.sum(jnp.where(chosen, 1.0, 0.0), axis=1, keepdims=True)
        ids = jnp.sum(jnp.where(chosen, number, 0.0), axis=1, keepdims=True)
        nexts = jnp.sum(jnp.where(chosen, follows, 0.0), axis=1, keepdims=True)
        ids = jnp.where(count > 0.5, ids, -1.0)
        nexts = jnp.where(count > 0.5, nexts, -2.0)
        place = iota((held, LANES), 0) == 2 * iota((held, LANES), 1) + k
        id_col = id_col + to_column(to_row(ids, square_eye), place)
        next_col = next_col + to_column(to_row(nexts, square_eye), place)
    held_eye = iota((held, held), 0) == iota((held, held), 1)
    id_row = to_row(id_col, held_eye)
    next_row = to_row(next_col, held_eye)
    y = [arrived_ref[c] for c in range(3)]
    nxt = pick_rows((next_col == id_row).astype(BF16), y)
    prv = pick_rows((id_col == next_row).astype(BF16), y)
    lane = iota((held, LANES), 1)
    arrays = []
    for c in range(3):
        v, nx, pv = y[c], nxt[c], prv[c]
        a1 = jnp.where(lane < LANES - 1, roll(v, -1), roll(nx, -1))
        a2 = jnp.where(lane < LANES - 2, roll(v, -2), roll(nx, -2))
        b1 = jnp.where(lane < 1, roll(pv, 1), roll(v, 1))
        b2 = jnp.where(lane < 2, roll(pv, 2), roll(v, 2))
        sm = (6.0 * v + 4.0 * (a1 + b1) + (a2 + b2)) * 0.0625
        smooth_ref[c] = sm
        after = (
            6.0 * roll(nx, -1) + 4.0 * (roll(nx, -2) + v) + (roll(nx, -3) + roll(v, 1))
        ) * 0.0625
        ahead = jnp.where(lane < LANES - 1, roll(sm, -1), after)
        arrays += [0.5 * (ahead + sm), ahead - sm]
    pick = jnp.zeros((8, LANES), jnp.bool_)
    for j, where in enumerate(EDGE_LANES):
        pick = jnp.logical_or(
            pick, jnp.logical_and(iota((8, LANES), 0) == j, iota((8, LANES), 1) == where)
        )
    stack = jnp.concatenate([part for array in arrays for part in three_parts(array)], axis=0)
    got = lax.dot_general(
        pick.astype(BF16), stack, (((1,), (1,)), ((), ())), preferred_element_type=F32
    )
    got = [
        got[:, 3 * m * held : (3 * m + 1) * held]
        + got[:, (3 * m + 1) * held : (3 * m + 2) * held]
        + got[:, (3 * m + 2) * held : (3 * m + 3) * held]
        for m in range(6)
    ]
    rows, highs, lows = features(got[0::2], got[1::2])
    for h in range(held // LANES):
        at = slice(h * LANES, (h + 1) * LANES)
        step = held // LANES
        for k, row in enumerate(rows):
            b_ref[pl.ds((slots + h) * 32 + k, 8, stride=32 * step), :] = row[:, at]
        for k in range(6):
            f_ref[pl.ds((slots + h) * 16 + k, 8, stride=16 * step), :] = highs[k][:, at]
            f_ref[pl.ds((slots + h) * 16 + 8 + k, 8, stride=16 * step), :] = lows[k][:, at]

    acc_ref[...] = jnp.zeros_like(acc_ref)
    used = slots + len(EDGE_LANES) * (held // LANES)
    a = a_ref[...].astype(BF16)

    def chunk(turn, carry):
        b_at = pl.multiple_of(turn * (CHUNK * 32), 32)
        f_at = pl.multiple_of(turn * (CHUNK * 16), 16)
        b = jnp.concatenate(
            [b_ref[pl.ds(b_at + 32 * j, 32), :].astype(BF16) for j in range(CHUNK)], axis=1
        )
        f = jnp.concatenate(
            [f_ref[pl.ds(f_at + 16 * j, 16), :].astype(BF16) for j in range(CHUNK)], axis=1
        )
        q = lax.dot_general(b, a, (((0,), (0,)), ((), ())), preferred_element_type=F32)
        r = lax.rsqrt(q)
        high, low = two_parts(r * r * r)
        acc_ref[...] += jnp.dot(f, high, preferred_element_type=F32) + jnp.dot(
            f, low, preferred_element_type=F32
        )
        return carry

    lax.fori_loop(0, used // CHUNK, chunk, 0)
    vel_ref[...] = jnp.zeros_like(vel_ref)
    for h in range(2):
        at = slice(h * half, (h + 1) * half)
        t = [tgt_ref[h * 3 + c : h * 3 + c + 1, :] for c in range(3)]
        s = [acc_ref[k : k + 1, at] + acc_ref[8 + k : 9 + k, at] for k in range(6)]
        vel_ref[0:1, at] = scale * (s[1] * t[2] - s[2] * t[1] - s[3])
        vel_ref[1:2, at] = scale * (s[2] * t[0] - s[0] * t[2] - s[4])
        vel_ref[2:3, at] = scale * (s[0] * t[1] - s[1] * t[0] - s[5])


def reduce_kernel(n_row, n_col, part_ref, out_ref, row_in, total, col_in, s1, r1, s2, r2):
    me_r = lax.axis_index("row")
    me_c = lax.axis_index("col")
    width = total.shape[1]
    first = []
    for step in range(1, n_row):
        to = lax.rem(me_r + step, n_row)
        copy = pltpu.make_async_remote_copy(
            src_ref=part_ref.at[:, pl.ds(pl.multiple_of(to * width, width), width)],
            dst_ref=row_in.at[me_r],
            send_sem=s1.at[step],
            recv_sem=r1.at[me_r],
            device_id=(to, me_c),
            device_id_type=MESH,
        )
        copy.start()
        first.append(copy)
    row_in[me_r] = part_ref[:, pl.ds(pl.multiple_of(me_r * width, width), width)]
    for step in range(1, n_row):
        frm = lax.rem(me_r + step, n_row)
        pltpu.make_async_copy(row_in.at[frm], row_in.at[frm], r1.at[frm]).wait()
    value = row_in[0]
    for r in range(1, n_row):
        value = value + row_in[r]
    total[...] = value
    second = []
    for step in range(1, n_col):
        to = lax.rem(me_c + step, n_col)
        copy = pltpu.make_async_remote_copy(
            src_ref=total,
            dst_ref=col_in.at[me_c],
            send_sem=s2.at[step],
            recv_sem=r2.at[me_c],
            device_id=(me_r, to),
            device_id_type=MESH,
        )
        copy.start()
        second.append(copy)
    col_in[me_c] = value
    for step in range(1, n_col):
        frm = lax.rem(me_c + step, n_col)
        pltpu.make_async_copy(col_in.at[frm], col_in.at[frm], r2.at[frm]).wait()
    value = col_in[0]
    for c in range(1, n_col):
        value = value + col_in[c]
    out_ref[...] = value
    for copy in first + second:
        copy.wait_send()


def shards(n_row, n_col, positions, block_links, panel_points):
    devices = n_row * n_col
    slots, block_len = positions.shape[1:]
    held = 2 * slots
    blocks = block_links.shape[1]
    groups, panel = panel_points.shape
    targets = groups * panel
    vmem = pl.BlockSpec(memory_space=pltpu.VMEM)
    smem = pl.BlockSpec(memory_space=pltpu.SMEM)
    hbm = pl.BlockSpec(memory_space=pl.ANY)
    params = pltpu.CompilerParams(vmem_limit_bytes=VMEM_LIMIT)
    remote = pltpu.CompilerParams(has_side_effects=True)
    me = lax.axis_index(("row", "col")).astype(jnp.int32).reshape(1)
    outgoing, partial_targets = pl.pallas_call(
        prep_kernel,
        out_shape=(
            jax.ShapeDtypeStruct((3, held, block_len), F32),
            jax.ShapeDtypeStruct((8, targets // 2), F32),
        ),
        in_specs=[smem, vmem, vmem, vmem],
        out_specs=(vmem, vmem),
        compiler_params=params,
        name="prep",
    )(me, positions, block_links, panel_points)
    width = targets // 2 // n_row
    dma = pltpu.SemaphoreType.DMA
    arrived, all_targets = pl.pallas_call(
        functools.partial(exchange_kernel, n_row, n_col),
        out_shape=(
            jax.ShapeDtypeStruct((3, devices, 2, block_len), F32),
            jax.ShapeDtypeStruct((8, targets // 2), F32),
        ),
        in_specs=[hbm, vmem],
        out_specs=(hbm, vmem),
        scratch_shapes=[
            pltpu.VMEM((n_row, 8, width), F32),
            pltpu.VMEM((8, width), F32),
            pltpu.VMEM((n_col, 8, width), F32),
            dma, dma, dma,
            dma((n_row,)), dma((n_row,)),
            dma((n_col,)), dma((n_col,)),
            dma((n_row,)), dma((n_row,)),
        ],
        compiler_params=remote,
        name="exchange",
    )(outgoing.reshape(3, devices, 2, block_len), partial_targets)
    stored = -(-(slots + 8 * (held // LANES)) // CHUNK) * CHUNK
    scale = 1.0 / (math.pi * math.sqrt(blocks * block_len))
    smoothed, partial_velocity = pl.pallas_call(
        functools.partial(velocity_kernel, scale),
        out_shape=(
            jax.ShapeDtypeStruct((3, held, block_len), F32),
            jax.ShapeDtypeStruct((8, targets), F32),
        ),
        in_specs=[smem, vmem, vmem, vmem, vmem],
        out_specs=(vmem, vmem),
        scratch_shapes=[
            pltpu.VMEM((stored * 32, LANES), F32),
            pltpu.VMEM((stored * 16, LANES), F32),
            pltpu.VMEM((32, targets), F32),
            pltpu.VMEM((16, targets), F32),
        ],
        compiler_params=params,
        name="velocity",
    )(
        me,
        positions,
        arrived.reshape(3, held, block_len),
        block_links.reshape(2, devices, slots),
        all_targets,
    )
    summed = pl.pallas_call(
        functools.partial(reduce_kernel, n_row, n_col),
        out_shape=jax.ShapeDtypeStruct((8, panel), F32),
        in_specs=[vmem],
        out_specs=vmem,
        scratch_shapes=[
            pltpu.VMEM((n_row, 8, panel), F32),
            pltpu.VMEM((8, panel), F32),
            pltpu.VMEM((n_col, 8, panel), F32),
            dma((n_row,)), dma((n_row,)),
            dma((n_col,)), dma((n_col,)),
        ],
        compiler_params=remote,
        name="reduce",
    )(partial_velocity)
    share = panel // n_col
    part = lax.dynamic_slice(summed, (0, lax.axis_index("col") * share), (3, share))
    return smoothed, part[None]


def solution(mesh):
    placed = (P(None, ("row", "col"), None), P(), P())
    return jax.shard_map(
        functools.partial(shards, mesh.shape["row"], mesh.shape["col"]),
        mesh=mesh,
        in_specs=placed,
        out_specs=(P(None, ("row", "col"), None), P("row", None, "col")),
        check_vma=False,
    )
```

time: 982 us -> 114 us (0.12)
  matrix products: 550 us -> 0 us
  local copies, waits for them, and re-layouts: 239 us -> 2.89 us
  blocking collectives: 114 us -> 0 us
  Pallas kernels: 0 us -> 110 us
  other arithmetic: 42.8 us -> 0 us
  between operations: 14.6 us -> 0.65 us
  starting transfers between devices: 11.6 us -> 0 us
    dot_general x32 -> x0, matrix products: 550 us -> none  [the longest x16 410 us: panel_sums(): lax.dot_general(targets, centres, (((0,), (0,)), ((), ())), precision=lax...]
    scatter x3 -> x0, local copies, waits for them, and re-layouts: 133 us -> none  [the longest x1 60.5 us: shards(): precedes = jnp.zeros_like(follows).at[follows].set(counter)]
    psum x2 -> x0, blocking collectives: 114 us -> none  [the longest x1 81 us: shards(): all_targets = lax.psum(local_targets, ('row', 'col'))]
    pallas_call x0 -> x4, Pallas kernels: none -> 110 us  [the longest x1 54.3 us: shards(): pl.pallas_call(functools.partial(velocity_kernel, scale), out_shape=(jax....]
    gather x17 -> x0, local copies, waits for them, and re-layouts: 71.3 us -> none  [the longest x2 32.6 us: shards(): picked = smoothed[:, places[wanted_block], wanted_point]]
    while x16 -> x0, other arithmetic: 17.1 us -> none
    add x2 -> x0, local copies, waits for them, and re-layouts: 17 us -> none  [smooth_loops(): points = points + SMOOTH_RATE * (behind - 2.0 * points + ahead)]
    sub x17 -> x0, other arithmetic: 16.5 us -> none  [cross_three(): left_vec[1] * right_vec[2] - left_vec[2] * right_vec[1]]
  transfers between devices with their start and end apart: 2 -> 0, of which waited for: 0 -> 0; matrix products, arithmetic and copies ran while one was open for 18% -> 0% of each run, Pallas kernels for 0% -> 0%
where the time goes in v1:
time: 114 us
  Pallas kernels  110 us (96%)
  local copies, waits for them, and re-layouts  2.89 us (3%)
    pallas_call x1, Pallas kernels, shards(): pl.pallas_call(functools.partial(velocity_kernel, scale), out_shape=(jax....  54.3 us
    pallas_call x1, Pallas kernels, shards(): pl.pallas_call(functools.partial(exchange_kernel, n_row, n_col), out_shap...  28.9 us
    pallas_call x1, Pallas kernels, shards(): pl.pallas_call(functools.partial(reduce_kernel, n_row, n_col), out_shape=...  20.5 us
    pallas_call x1, Pallas kernels, shards(): pl.pallas_call(prep_kernel, out_shape=(jax.ShapeDtypeStruct((3, held, blo...  6.2 us

profile of v1, /device:TPU:1, one launch (start us, length us, event | category | flops | bytes accessed | tf_op | source)
XLA Modules:
  0.0 113.5 jit_solution(6963872519054776368)
XLA Ops:
  0.6 1.6 %copy.8 = s32[1,2,128,128]{3,2,1,0:T(8,128)} copy(s32[1,2,128,128]{3,1,2,0:T(2,128)} %bitcast.10) | data formatting | bytes 262144
  2.2 6.2 %prep.1 = (f32[3,256,128]{2,1,0:T(8,128)}, f32[8,1024]{1,0:T(8,128)}) custom-call(s32[1]{0:T(128)} %bitcast.me_ref, f32[3,128,128]{2,1,0:T(8,128)} %pos_ref.3, s32[2,16384]{1,0:T(2,128)} %links_ref.1, s32[8,256]{1,0:T(8,128)} %panel_ref.1), custom_call_target="tpu_custom_call" | custom-call | tf_op jit(solution)/shard_map/prep/pallas_call | solution.py:458
  8.4 28.9 %exchange.1 = (f32[3,128,2,128]{3,2,1,0:T(2,128)}, f32[8,1024]{1,0:T(8,128)}) custom-call(f32[3,128,2,128]{3,2,1,0:T(2,128)} %bitcast.12, f32[8,1024]{1,0:T(8,128)} %get-tuple-element.9.part_ref), custom_call_target="tpu_custom_call" | custom-call | tf_op jit(solution)/shard_map/exchange/pallas_call | solution.py:471
  37.3 54.3 %velocity.1 = (f32[3,256,128]{2,1,0:T(8,128)}, f32[8,2048]{1,0:T(8,128)}) custom-call(s32[1]{0:T(128)} %bitcast.me_ref, f32[3,128,128]{2,1,0:T(8,128)} %pos_ref.3, f32[3,256,128]{2,1,0:T(8,128)} %bitcast.11, s32[2,128,128]{2,1,0:T(8,128)} %bitcast.9, f32[8,1024]{1,0:T(8,128)} %get-tuple-element.11.tgt_ref), custom_call_target="tpu_custom_call" | custom-call | tf_op jit(solution)/shard_map/velocity/pallas_call | solution.py:493
  91.7 20.5 %reduce.1 = f32[8,256]{1,0:T(8,128)} custom-call(f32[8,2048]{1,0:T(8,128)} %get-tuple-element.13.part_ref), custom_call_target="tpu_custom_call" | custom-call | tf_op jit(solution)/shard_map/reduce/pallas_call | solution.py:516
  112.2 0.8 dynamic-slice_bitcast_fusion
  113.0 0.6 copy.5

commit v2 on v0

v2 whole, which is shorter than its diff:
```python
import functools
import math

import jax
import jax.numpy as jnp
from jax import lax
from jax.experimental import pallas as pl
from jax.experimental.pallas import tpu as pltpu
from jax.sharding import PartitionSpec as P

CORE_SQUARED = 0.01
F32 = jnp.float32
BF16 = jnp.bfloat16
LANES = 128
VMEM_LIMIT = 56 << 20
MESH = pl.DeviceIdType.MESH
CHUNK = 8
EDGE_LANES = (125, 126, 127, 0, 1)


def iota(shape, axis):
    return lax.broadcasted_iota(jnp.int32, shape, axis)


def three_parts(value):
    high = value.astype(BF16)
    rest = value - high.astype(F32)
    middle = rest.astype(BF16)
    return high, middle, (rest - middle.astype(F32)).astype(BF16)


def two_parts(value):
    high = value.astype(BF16)
    return high, (value - high.astype(F32)).astype(BF16)


def to_column(row, eye):
    return jnp.sum(jnp.where(eye, row, 0.0), axis=1, keepdims=True)


def to_row(column, eye):
    return jnp.sum(jnp.where(eye, column, 0.0), axis=0, keepdims=True)


def pick_rows(chooser, arrays):
    width = arrays[0].shape[1]
    parts = jnp.concatenate([part for array in arrays for part in three_parts(array)], axis=1)
    got = jnp.dot(chooser, parts, preferred_element_type=F32)
    result = []
    for n in range(len(arrays)):
        at = 3 * n * width
        result.append(
            got[:, at : at + width]
            + got[:, at + width : at + 2 * width]
            + got[:, at + 2 * width : at + 3 * width]
        )
    return result


def roll(value, shift):
    return pltpu.roll(value, shift % LANES, 1)


def features(centres, segments):
    rows = []
    for c in centres:
        high, middle, low = (part.astype(F32) for part in three_parts(c))
        rows += [high, middle, high, low, high, middle]
    square = centres[0] * centres[0] + centres[1] * centres[1] + centres[2] * centres[2]
    rows += [part.astype(F32) for part in three_parts(square)]
    rows += [jnp.ones_like(square)] * 3
    s, c = segments, centres
    six = [s[0], s[1], s[2]]
    six += [s[1] * c[2] - s[2] * c[1], s[2] * c[0] - s[0] * c[2], s[0] * c[1] - s[1] * c[0]]
    pairs = [two_parts(value) for value in six]
    return rows, [pair[0].astype(F32) for pair in pairs], [pair[1].astype(F32) for pair in pairs]


def step_kernel(
    n_row, n_col, scale, pos_ref, links_ref, panel_ref, smooth_ref, vel_ref,
    grid_ref, part_ref, tgt_ref, send_ref, arrived_ref, b_ref, f_ref, a_ref, acc_ref,
    pair_ref, sum_ref, row_in, total, col_in, row_sum, row_total, col_sum,
    send_sem, recv_sem, s1, r1, s2, r2, s3, r3, s4, r4, s5, r5,
):
    me_r = lax.axis_index("row")
    me_c = lax.axis_index("col")
    me = me_r * n_col + me_c
    n = n_row * n_col
    slots = pos_ref.shape[1]
    held = 2 * n

    barrier = pltpu.get_barrier_semaphore()
    for step in range(1, n_row):
        to = lax.rem(me_r + step, n_row)
        pl.semaphore_signal(barrier, inc=1, device_id=(to, me_c), device_id_type=MESH)
    for step in range(1, n_col):
        to = lax.rem(me_c + step, n_col)
        pl.semaphore_signal(barrier, inc=1, device_id=(me_r, to), device_id_type=MESH)

    def send_row(source, target, send, recv):
        copies = []
        for step in range(1, n_row):
            to = lax.rem(me_r + step, n_row)
            copy = pltpu.make_async_remote_copy(
                src_ref=source(to),
                dst_ref=target(me_r),
                send_sem=send.at[step],
                recv_sem=recv.at[me_r],
                device_id=(to, me_c),
                device_id_type=MESH,
            )
            copy.start()
            copies.append(copy)
        return copies

    def send_col(source, target, send, recv):
        copies = []
        for step in range(1, n_col):
            to = lax.rem(me_c + step, n_col)
            copy = pltpu.make_async_remote_copy(
                src_ref=source,
                dst_ref=target(me_c),
                send_sem=send.at[step],
                recv_sem=recv.at[me_c],
                device_id=(me_r, to),
                device_id_type=MESH,
            )
            copy.start()
            copies.append(copy)
        return copies

    def wait_from(mine, count, target, recv):
        for step in range(1, count):
            frm = lax.rem(mine + step, count)
            pltpu.make_async_copy(target(frm), target(frm), recv.at[frm]).wait()

    def add_up(ref, count):
        value = ref[0]
        for r in range(1, count):
            value = value + ref[r]
        return value

    eye = iota((slots, LANES), 0) == iota((slots, LANES), 1)
    here = pl.ds(pl.multiple_of(me * slots, LANES), LANES)
    owner_row = links_ref[0:1, here].astype(F32)
    follow_row = links_ref[1:2, here].astype(F32)
    follow_col = to_column(follow_row, eye)
    mine_col = (me * slots + iota((slots, 1), 0)).astype(F32)
    lane_row = iota((1, LANES), 1).astype(F32)

    def look(turn, found):
        at = pl.multiple_of(turn * LANES, LANES)
        row = links_ref[1:2, pl.ds(at, LANES)].astype(F32)
        grid_ref[1, pl.ds(turn, 1), :] = row
        grid_ref[0, pl.ds(turn, 1), :] = links_ref[0:1, pl.ds(at, LANES)].astype(F32)
        number = lane_row + (turn * LANES).astype(F32)
        return found + jnp.where(row == mine_col, number, 0.0)

    precede_col = jnp.sum(
        lax.fori_loop(0, n, look, jnp.zeros((slots, LANES), F32), unroll=8),
        axis=1,
        keepdims=True,
    )
    raw = [pos_ref[c] for c in range(3)]
    lane = iota((slots, LANES), 1)
    rows = []
    for x in raw:
        b1, b2, a1, a2 = roll(x, 1), roll(x, 2), roll(x, -1), roll(x, -2)
        zero = jnp.zeros_like(x)
        wrap = (
            4.0 * (jnp.where(lane < 1, b1, zero) + jnp.where(lane > LANES - 2, a1, zero))
            + (jnp.where(lane < 2, b2, zero) + jnp.where(lane > LANES - 3, a2, zero))
        )
        inside = (
            6.0 * x
            + 4.0 * (jnp.where(lane < 1, zero, b1) + jnp.where(lane > LANES - 2, zero, a1))
            + (jnp.where(lane < 2, zero, b2) + jnp.where(lane > LANES - 3, zero, a2))
        )
        rows += [inside * 0.0625, wrap * 0.0625]
    stack = jnp.concatenate(rows, axis=0)
    parts = jnp.concatenate(three_parts(stack), axis=0)
    high = stack.shape[0]
    panel = panel_ref.shape[1]
    half = tgt_ref.shape[1]
    per_half = half // panel
    part_ref[...] = jnp.zeros_like(part_ref)
    for r in range(panel_ref.shape[0]):
        flat = panel_ref[r : r + 1, :]
        block = (flat // LANES).astype(F32)
        point = flat % LANES
        one_point = (iota((LANES, panel), 0) == point).astype(BF16)
        got = jnp.dot(parts, one_point, preferred_element_type=F32)
        got = got[:high] + got[high : 2 * high] + got[2 * high :]
        here_mask = block == mine_col
        edge_mask = jnp.logical_or(
            jnp.logical_and(precede_col == block, point >= LANES - 2),
            jnp.logical_and(follow_col == block, point <= 1),
        )
        for c in range(3):
            at = 2 * c * slots
            value = jnp.where(here_mask, got[at : at + slots], 0.0) + jnp.where(
                edge_mask, got[at + slots : at + 2 * slots], 0.0
            )
            row = (r // per_half) * 3 + c
            col = (r % per_half) * panel
            part_ref[row : row + 1, col : col + panel] = jnp.sum(value, axis=0, keepdims=True)

    width = half // n_row

    def piece(ref, r, size):
        return ref.at[:, pl.ds(pl.multiple_of(r * size, size), size)]

    pl.semaphore_wait(barrier, n_row + n_col - 2)
    copies = send_row(lambda to: piece(part_ref, to, width), lambda r: row_in.at[r], s1, r1)
    row_in[me_r] = part_ref[:, pl.ds(pl.multiple_of(me_r * width, width), width)]

    owner_col = to_column(owner_row, eye)
    earlier = iota((slots, LANES), 0) < iota((slots, LANES), 1)
    same = jnp.logical_and(owner_col == owner_row, earlier)
    rank_row = jnp.sum(jnp.where(same, 1.0, 0.0), axis=0, keepdims=True)
    send_ref[...] = jnp.zeros_like(send_ref)
    to_owner = iota((n, LANES), 0).astype(F32) == owner_row
    for k in range(2):
        chooser = jnp.logical_and(to_owner, rank_row == float(k)).astype(BF16)
        for c, moved in enumerate(pick_rows(chooser, raw)):
            send_ref[pl.ds(2 * c + k, n, stride=8), :] = moved

    wait_from(me_r, n_row, lambda r: row_in.at[r], r1)
    value = add_up(row_in, n_row)
    total[...] = value
    copies += send_col(total, lambda c: col_in.at[c], s2, r2)
    col_in[me_c] = value

    b_ref[...] = jnp.zeros_like(b_ref)
    f_ref[...] = jnp.zeros_like(f_ref)
    inner = jnp.logical_and(lane >= 2, lane < LANES - 3)
    centres, segments = [], []
    for x in raw:
        sm = (6.0 * x + 4.0 * (roll(x, 1) + roll(x, -1)) + (roll(x, 2) + roll(x, -2))) * 0.0625
        ahead = roll(sm, -1)
        segments.append(jnp.where(inner, ahead - sm, 0.0))
        centres.append(0.5 * (ahead + sm))
    rows, highs, lows = features(centres, segments)
    for k, row in enumerate(rows):
        b_ref[pl.ds(k, slots, stride=32), :] = row
    for k in range(6):
        f_ref[pl.ds(k, slots, stride=16), :] = highs[k]
        f_ref[pl.ds(8 + k, slots, stride=16), :] = lows[k]

    wait_from(me_c, n_col, lambda c: col_in.at[c], r2)
    value = add_up(col_in, n_col)
    tgt_ref[:, pl.ds(pl.multiple_of(me_r * width, width), width)] = value
    copies += send_row(
        lambda to: piece(tgt_ref, me_r, width), lambda r: piece(tgt_ref, r, width), s3, r3
    )

    number = (iota((n, LANES), 0) * LANES + iota((n, LANES), 1)).astype(F32)
    mine = grid_ref[0] == me.astype(F32)
    before = (iota((LANES, LANES), 0) < iota((LANES, LANES), 1)).astype(BF16)
    rank = jnp.dot(mine.astype(BF16), before, preferred_element_type=F32)
    ids, nexts, id_rows, next_rows = [], [], [], []
    for k in range(2):
        chosen = jnp.logical_and(mine, rank == float(k))
        count = jnp.sum(jnp.where(chosen, 1.0, 0.0), axis=1, keepdims=True)
        one = jnp.sum(jnp.where(chosen, number, 0.0), axis=1, keepdims=True)
        two = jnp.sum(jnp.where(chosen, grid_ref[1], 0.0), axis=1, keepdims=True)
        ids.append(jnp.where(count > 0.5, one, -1.0))
        nexts.append(jnp.where(count > 0.5, two, -2.0))
        id_rows.append(to_row(ids[k], eye))
        next_rows.append(to_row(nexts[k], eye))
    for k in range(2):
        for m in range(2):
            at = (slice(k * n, (k + 1) * n), slice(m * n, (m + 1) * n))
            pair_ref[0, at[0], at[1]] = jnp.where(nexts[k] == id_rows[m], 1.0, 0.0)
            pair_ref[1, at[0], at[1]] = jnp.where(ids[k] == next_rows[m], 1.0, 0.0)

    wait_from(me_r, n_row, lambda r: piece(tgt_ref, r, width), r3)
    for copy in copies:
        copy.wait_send()

    a_ref[...] = jnp.zeros_like(a_ref)
    for h in range(2):
        at = slice(h * half, (h + 1) * half)
        t = [tgt_ref[h * 3 + c : h * 3 + c + 1, :] for c in range(3)]
        rows = []
        for value in t:
            top, middle, low = (part.astype(F32) for part in three_parts(-2.0 * value))
            rows += [top, top, middle, top, low, middle]
        rows += [jnp.ones_like(t[0])] * 3
        square = t[0] * t[0] + t[1] * t[1] + t[2] * t[2] + CORE_SQUARED
        rows += [part.astype(F32) for part in three_parts(square)]
        for k, row in enumerate(rows):
            a_ref[k : k + 1, at] = row

    acc_ref[...] = jnp.zeros_like(acc_ref)
    a = a_ref[...].astype(BF16)

    def add_blocks(first, count):
        b_at = pl.multiple_of(first * 32, 32)
        f_at = pl.multiple_of(first * 16, 16)
        b = jnp.concatenate(
            [b_ref[pl.ds(b_at + 32 * j, 32), :].astype(BF16) for j in range(count)], axis=1
        )
        f = jnp.concatenate(
            [f_ref[pl.ds(f_at + 16 * j, 16), :].astype(BF16) for j in range(count)], axis=1
        )
        q = lax.dot_general(b, a, (((0,), (0,)), ((), ())), preferred_element_type=F32)
        r = lax.rsqrt(q)
        top, low = two_parts(r * r * r)
        acc_ref[...] += jnp.dot(f, top, preferred_element_type=F32) + jnp.dot(
            f, low, preferred_element_type=F32
        )

    def tile(ref, device):
        return ref.at[pl.ds(pl.multiple_of(device * 8, 8), 8), :]

    def start_block(step, carry):
        to = lax.rem(me + step, n)
        pltpu.make_async_remote_copy(
            src_ref=tile(send_ref, to),
            dst_ref=tile(arrived_ref, me),
            send_sem=send_sem,
            recv_sem=recv_sem,
            device_id=(to // n_col, lax.rem(to, n_col)),
            device_id_type=MESH,
        ).start()
        return carry

    turns = slots // CHUNK
    each = n // turns
    own = pl.ds(pl.multiple_of(me * 8, 8), 8)
    arrived_ref[own, :] = send_ref[own, :]
    lax.fori_loop(1, each, start_block, 0)

    def chunk(turn, carry):
        lax.fori_loop((turn + 1) * each, (turn + 2) * each, start_block, 0)
        add_blocks(turn * CHUNK, CHUNK)
        return carry

    lax.fori_loop(0, turns - 1, chunk, 0)
    add_blocks((turns - 1) * CHUNK, CHUNK)

    rest = pl.ds(0, 8 * (n - 1))
    pltpu.make_async_copy(arrived_ref.at[rest], arrived_ref.at[rest], recv_sem).wait()
    pltpu.make_async_copy(send_ref.at[rest], send_ref.at[rest], send_sem).wait()

    y = [
        jnp.concatenate(
            [arrived_ref[pl.ds(2 * c + k, n, stride=8), :] for k in range(2)], axis=0
        )
        for c in range(3)
    ]
    nxt = pick_rows(pair_ref[0].astype(BF16), y)
    prv = pick_rows(pair_ref[1].astype(BF16), y)
    lane = iota((held, LANES), 1)
    arrays = []
    for c in range(3):
        v, nx, pv = y[c], nxt[c], prv[c]
        a1 = jnp.where(lane < LANES - 1, roll(v, -1), roll(nx, -1))
        a2 = jnp.where(lane < LANES - 2, roll(v, -2), roll(nx, -2))
        b1 = jnp.where(lane < 1, roll(pv, 1), roll(v, 1))
        b2 = jnp.where(lane < 2, roll(pv, 2), roll(v, 2))
        sm = (6.0 * v + 4.0 * (a1 + b1) + (a2 + b2)) * 0.0625
        for k in range(2):
            smooth_ref[c, pl.ds(k, n, stride=2), :] = sm[k * n : (k + 1) * n]
        after = (
            6.0 * roll(nx, -1) + 4.0 * (roll(nx, -2) + v) + (roll(nx, -3) + roll(v, 1))
        ) * 0.0625
        ahead = jnp.where(lane < LANES - 1, roll(sm, -1), after)
        arrays += [0.5 * (ahead + sm), ahead - sm]
    pick = jnp.zeros((8, LANES), F32)
    for j, where in enumerate(EDGE_LANES):
        hit = jnp.logical_and(iota((8, LANES), 0) == j, iota((8, LANES), 1) == where)
        pick = pick + jnp.where(hit, 1.0, 0.0)
    stack = jnp.concatenate([part for array in arrays for part in three_parts(array)], axis=0)
    got = lax.dot_general(
        pick.astype(BF16), stack, (((1,), (1,)), ((), ())), preferred_element_type=F32
    )
    got = [
        got[:, 3 * m * held : (3 * m + 1) * held]
        + got[:, (3 * m + 1) * held : (3 * m + 2) * held]
        + got[:, (3 * m + 2) * held : (3 * m + 3) * held]
        for m in range(6)
    ]
    rows, highs, lows = features(got[0::2], got[1::2])
    for k in range(2):
        at = slice(k * n, (k + 1) * n)
        for m, row in enumerate(rows):
            b_ref[pl.ds((slots + k) * 32 + m, 8, stride=64), :] = row[:, at]
        for m in range(6):
            f_ref[pl.ds((slots + k) * 16 + m, 8, stride=32), :] = highs[m][:, at]
            f_ref[pl.ds((slots + k) * 16 + 8 + m, 8, stride=32), :] = lows[m][:, at]
    add_blocks(slots, 2 * len(EDGE_LANES))

    sum_ref[...] = jnp.zeros_like(sum_ref)
    for h in range(2):
        at = slice(h * half, (h + 1) * half)
        t = [tgt_ref[h * 3 + c : h * 3 + c + 1, :] for c in range(3)]
        s = [acc_ref[k : k + 1, at] + acc_ref[8 + k : 9 + k, at] for k in range(6)]
        sum_ref[0:1, at] = scale * (s[1] * t[2] - s[2] * t[1] - s[3])
        sum_ref[1:2, at] = scale * (s[2] * t[0] - s[0] * t[2] - s[4])
        sum_ref[2:3, at] = scale * (s[0] * t[1] - s[1] * t[0] - s[5])
    copies = send_row(lambda to: piece(sum_ref, to, panel), lambda r: row_sum.at[r], s4, r4)
    row_sum[me_r] = sum_ref[:, pl.ds(pl.multiple_of(me_r * panel, panel), panel)]
    wait_from(me_r, n_row, lambda r: row_sum.at[r], r4)
    value = add_up(row_sum, n_row)
    row_total[...] = value
    copies += send_col(row_total, lambda c: col_sum.at[c], s5, r5)
    col_sum[me_c] = value
    wait_from(me_c, n_col, lambda c: col_sum.at[c], r5)
    value = add_up(col_sum, n_col)
    share = vel_ref.shape[1]
    pick = (iota((panel, share), 0) == me_c * share + iota((panel, share), 1)).astype(BF16)
    got = [jnp.dot(part, pick, preferred_element_type=F32) for part in three_parts(value)]
    vel_ref[...] = (got[0] + got[1] + got[2])[:3]
    for copy in copies:
        copy.wait_send()


def shards(n_row, n_col, positions, block_links, panel_points):
    devices = n_row * n_col
    slots, block_len = positions.shape[1:]
    held = 2 * devices
    blocks = block_links.shape[1]
    groups, panel = panel_points.shape
    targets = groups * panel
    width = targets // 2 // n_row
    stored = slots + 2 * 8
    scale = 1.0 / (math.pi * math.sqrt(blocks * block_len))
    whole = pl.BlockSpec(memory_space=pltpu.VMEM)
    dma = pltpu.SemaphoreType.DMA
    smoothed, velocity = pl.pallas_call(
        functools.partial(step_kernel, n_row, n_col, scale),
        out_shape=(
            jax.ShapeDtypeStruct((3, held, block_len), F32),
            jax.ShapeDtypeStruct((3, panel // n_col), F32),
        ),
        in_specs=[whole, whole, whole],
        out_specs=(whole, whole),
        scratch_shapes=[
            pltpu.VMEM((2, devices, slots), F32),
            pltpu.VMEM((8, targets // 2), F32),
            pltpu.VMEM((8, targets // 2), F32),
            pltpu.VMEM((8 * devices, block_len), F32),
            pltpu.VMEM((8 * devices, block_len), F32),
            pltpu.VMEM((stored * 32, LANES), F32),
            pltpu.VMEM((stored * 16, LANES), F32),
            pltpu.VMEM((32, targets), F32),
            pltpu.VMEM((16, targets), F32),
            pltpu.VMEM((2, held, held), F32),
            pltpu.VMEM((8, targets), F32),
            pltpu.VMEM((n_row, 8, width), F32),
            pltpu.VMEM((8, width), F32),
            pltpu.VMEM((n_col, 8, width), F32),
            pltpu.VMEM((n_row, 8, panel), F32),
            pltpu.VMEM((8, panel), F32),
            pltpu.VMEM((n_col, 8, panel), F32),
            dma, dma,
            dma((n_row,)), dma((n_row,)),
            dma((n_col,)), dma((n_col,)),
            dma((n_row,)), dma((n_row,)),
            dma((n_row,)), dma((n_row,)),
            dma((n_col,)), dma((n_col,)),
        ],
        compiler_params=pltpu.CompilerParams(
            vmem_limit_bytes=VMEM_LIMIT, collective_id=0, has_side_effects=True
        ),
        name="step",
    )(positions, block_links, panel_points)
    return smoothed, velocity[None]


def solution(mesh):
    placed = (P(None, ("row", "col"), None), P(), P())
    return jax.shard_map(
        functools.partial(shards, mesh.shape["row"], mesh.shape["col"]),
        mesh=mesh,
        in_specs=placed,
        out_specs=(P(None, ("row", "col"), None), P("row", None, "col")),
        check_vma=False,
    )
```

time: 982 us -> 89.2 us (0.09)
  matrix products: 550 us -> 0 us
  local copies, waits for them, and re-layouts: 239 us -> 3 us
  blocking collectives: 114 us -> 0 us
  Pallas kernels: 0 us -> 85.3 us
  other arithmetic: 42.8 us -> 0 us
  between operations: 14.6 us -> 0.65 us
  starting transfers between devices: 11.6 us -> 0 us
    dot_general x32 -> x0, matrix products: 550 us -> none  [the longest x16 410 us: panel_sums(): lax.dot_general(targets, centres, (((0,), (0,)), ((), ())), precision=lax...]
    scatter x3 -> x0, local copies, waits for them, and re-layouts: 133 us -> none  [the longest x1 60.5 us: shards(): precedes = jnp.zeros_like(follows).at[follows].set(counter)]
    psum x2 -> x0, blocking collectives: 114 us -> none  [the longest x1 81 us: shards(): all_targets = lax.psum(local_targets, ('row', 'col'))]
    pallas_call x0 -> x1, Pallas kernels: none -> 85.3 us  [shards(): pl.pallas_call(functools.partial(step_kernel, n_row, n_col, scale), out_s...]
    gather x17 -> x0, local copies, waits for them, and re-layouts: 71.3 us -> none  [the longest x2 32.6 us: shards(): picked = smoothed[:, places[wanted_block], wanted_point]]
    while x16 -> x0, other arithmetic: 17.1 us -> none
    add x2 -> x0, local copies, waits for them, and re-layouts: 17 us -> none  [smooth_loops(): points = points + SMOOTH_RATE * (behind - 2.0 * points + ahead)]
    sub x17 -> x0, other arithmetic: 16.5 us -> none  [cross_three(): left_vec[1] * right_vec[2] - left_vec[2] * right_vec[1]]
  transfers between devices with their start and end apart: 2 -> 0, of which waited for: 0 -> 0; matrix products, arithmetic and copies ran while one was open for 18% -> 0% of each run, Pallas kernels for 0% -> 0%
where the time goes in v2:
time: 89.2 us; the launch traced here: 89 us
  Pallas kernels  85.3 us (96%)
  local copies, waits for them, and re-layouts  3 us (3%)
    pallas_call x1, Pallas kernels, shards(): pl.pallas_call(functools.partial(step_kernel, n_row, n_col, scale), out_s...  85.3 us
    unnamed x4, local copies, waits for them, and re-layouts  3 us

profile of v2, /device:TPU:1, one launch (start us, length us, event | category | flops | bytes accessed | tf_op | source)
XLA Modules:
  0.0 89.0 jit_solution(9991646490403664496)
XLA Ops:
  0.6 85.3 %step.1 = (f32[3,256,128]{2,1,0:T(8,128)}, f32[3,16]{1,0:T(4,128)}) custom-call(f32[3,128,128]{2,1,0:T(8,128)} %pos_ref.1, s32[2,16384]{1,0:T(2,128)} %links_ref.1, s32[8,256]{1,0:T(8,128)} %panel_ref.1), custom_call_target="tpu_custom_call" | custom-call | tf_op jit(solution)/shard_map/step/pallas_call | solution.py:432
  85.9 0.0 copy-start
  86.0 0.7 copy-done
  86.6 0.6 copy.5
  87.2 1.8 %copy.7 = f32[3,256,128]{2,1,0:T(8,128)} copy(f32[3,256,128]{2,1,0:T(8,128)} %get-tuple-element.10) | data formatting | bytes 786432
Async XLA Ops:
  85.9 0.7 copy-start

commit v3 on v2

--- a/solution.py
+++ b/solution.py
@@ -14,7 +14,8 @@
 LANES = 128
 VMEM_LIMIT = 56 << 20
 MESH = pl.DeviceIdType.MESH
-CHUNK = 8
+CHUNK = 32
+TILE = 256
 EDGE_LANES = (125, 126, 127, 0, 1)
 
 
@@ -55,6 +56,24 @@
             + got[:, at + 2 * width : at + 3 * width]
         )
     return result
+
+
+def pick_lanes(lanes, arrays):
+    rows = arrays[0].shape[0]
+    pick = jnp.zeros((8, LANES), F32)
+    for j, where in enumerate(lanes):
+        hit = jnp.logical_and(iota((8, LANES), 0) == j, iota((8, LANES), 1) == where)
+        pick = pick + jnp.where(hit, 1.0, 0.0)
+    stack = jnp.concatenate([part for array in arrays for part in three_parts(array)], axis=0)
+    got = lax.dot_general(
+        pick.astype(BF16), stack, (((1,), (1,)), ((), ())), preferred_element_type=F32
+    )
+    return [
+        got[:, 3 * m * rows : (3 * m + 1) * rows]
+        + got[:, (3 * m + 1) * rows : (3 * m + 2) * rows]
+        + got[:, (3 * m + 2) * rows : (3 * m + 3) * rows]
+        for m in range(len(arrays))
+    ]
 
 
 def roll(value, shift):
@@ -80,7 +99,7 @@
     n_row, n_col, scale, pos_ref, links_ref, panel_ref, smooth_ref, vel_ref,
     grid_ref, part_ref, tgt_ref, send_ref, arrived_ref, b_ref, f_ref, a_ref, acc_ref,
     pair_ref, sum_ref, row_in, total, col_in, row_sum, row_total, col_sum,
-    send_sem, recv_sem, s1, r1, s2, r2, s3, r3, s4, r4, s5, r5,
+    held_ref, out_sem, send_sem, recv_sem, s1, r1, s2, r2, s3, r3, s4, r4, s5, r5,
 ):
     me_r = lax.axis_index("row")
     me_c = lax.axis_index("col")
@@ -163,7 +182,7 @@
     )
     raw = [pos_ref[c] for c in range(3)]
     lane = iota((slots, LANES), 1)
-    rows = []
+    inside, wraps = [], []
     for x in raw:
         b1, b2, a1, a2 = roll(x, 1), roll(x, 2), roll(x, -1), roll(x, -2)
         zero = jnp.zeros_like(x)
@@ -171,19 +190,23 @@
             4.0 * (jnp.where(lane < 1, b1, zero) + jnp.where(lane > LANES - 2, a1, zero))
             + (jnp.where(lane < 2, b2, zero) + jnp.where(lane > LANES - 3, a2, zero))
         )
-        inside = (
+        within = (
             6.0 * x
             + 4.0 * (jnp.where(lane < 1, zero, b1) + jnp.where(lane > LANES - 2, zero, a1))
             + (jnp.where(lane < 2, zero, b2) + jnp.where(lane > LANES - 3, zero, a2))
         )
-        rows += [inside * 0.0625, wrap * 0.0625]
-    stack = jnp.concatenate(rows, axis=0)
-    parts = jnp.concatenate(three_parts(stack), axis=0)
-    high = stack.shape[0]
+        inside.append(within * 0.0625)
+        wraps.append(wrap * 0.0625)
+    parts = jnp.concatenate(three_parts(jnp.concatenate(inside, axis=0)), axis=0)
+    high = 3 * slots
+    edges = pick_lanes((LANES - 2, LANES - 1, 0, 1), wraps)
+    edge_parts = jnp.concatenate([part for edge in edges for part in three_parts(edge)], axis=0)
     panel = panel_ref.shape[1]
     half = tgt_ref.shape[1]
     per_half = half // panel
     part_ref[...] = jnp.zeros_like(part_ref)
+    kind = iota((8, panel), 0)
+    edge_point = jnp.where(kind < 2, kind + (LANES - 2), jnp.where(kind < 4, kind - 2, -1))
     for r in range(panel_ref.shape[0]):
         flat = panel_ref[r : r + 1, :]
         block = (flat // LANES).astype(F32)
@@ -192,18 +215,23 @@
         got = jnp.dot(parts, one_point, preferred_element_type=F32)
         got = got[:high] + got[high : 2 * high] + got[2 * high :]
         here_mask = block == mine_col
-        edge_mask = jnp.logical_or(
-            jnp.logical_and(precede_col == block, point >= LANES - 2),
-            jnp.logical_and(follow_col == block, point <= 1),
-        )
+        over = jnp.dot(
+            edge_parts, (precede_col == block).astype(BF16), preferred_element_type=F32
+        )
+        under = jnp.dot(
+            edge_parts, (follow_col == block).astype(BF16), preferred_element_type=F32
+        )
+        beyond = jnp.where(lax.rem(iota(over.shape, 0), 8) < 2, over, under)
         for c in range(3):
-            at = 2 * c * slots
-            value = jnp.where(here_mask, got[at : at + slots], 0.0) + jnp.where(
-                edge_mask, got[at + slots : at + 2 * slots], 0.0
+            inner = jnp.where(here_mask, got[c * slots : (c + 1) * slots], 0.0)
+            outer = beyond[24 * c : 24 * c + 8]
+            outer = outer + beyond[24 * c + 8 : 24 * c + 16] + beyond[24 * c + 16 : 24 * c + 24]
+            value = jnp.sum(inner, axis=0, keepdims=True) + jnp.sum(
+                jnp.where(edge_point == point, outer, 0.0), axis=0, keepdims=True
             )
             row = (r // per_half) * 3 + c
             col = (r % per_half) * panel
-            part_ref[row : row + 1, col : col + panel] = jnp.sum(value, axis=0, keepdims=True)
+            part_ref[row : row + 1, col : col + panel] = value
 
     width = half // n_row
 
@@ -293,7 +321,6 @@
             a_ref[k : k + 1, at] = row
 
     acc_ref[...] = jnp.zeros_like(acc_ref)
-    a = a_ref[...].astype(BF16)
 
     def add_blocks(first, count):
         b_at = pl.multiple_of(first * 32, 32)
@@ -304,17 +331,19 @@
         f = jnp.concatenate(
             [f_ref[pl.ds(f_at + 16 * j, 16), :].astype(BF16) for j in range(count)], axis=1
         )
-        q = lax.dot_general(b, a, (((0,), (0,)), ((), ())), preferred_element_type=F32)
-        r = lax.rsqrt(q)
-        top, low = two_parts(r * r * r)
-        acc_ref[...] += jnp.dot(f, top, preferred_element_type=F32) + jnp.dot(
-            f, low, preferred_element_type=F32
-        )
+        for at in range(0, acc_ref.shape[1], TILE):
+            a = a_ref[:, at : at + TILE].astype(BF16)
+            q = lax.dot_general(b, a, (((0,), (0,)), ((), ())), preferred_element_type=F32)
+            r = lax.rsqrt(q)
+            top, low = two_parts(r * r * r)
+            acc_ref[:, at : at + TILE] += jnp.dot(f, top, preferred_element_type=F32) + jnp.dot(
+                f, low, preferred_element_type=F32
+            )
 
     def tile(ref, device):
         return ref.at[pl.ds(pl.multiple_of(device * 8, 8), 8), :]
 
-    def start_block(step, carry):
+    def start_block(step):
         to = lax.rem(me + step, n)
         pltpu.make_async_remote_copy(
             src_ref=tile(send_ref, to),
@@ -324,16 +353,17 @@
             device_id=(to // n_col, lax.rem(to, n_col)),
             device_id_type=MESH,
         ).start()
-        return carry
 
     turns = slots // CHUNK
-    each = n // turns
+    each = (n - 1) // (turns - 1)
     own = pl.ds(pl.multiple_of(me * 8, 8), 8)
     arrived_ref[own, :] = send_ref[own, :]
-    lax.fori_loop(1, each, start_block, 0)
+    for step in range(each * (turns - 1) + 1, n):
+        start_block(step)
 
     def chunk(turn, carry):
-        lax.fori_loop((turn + 1) * each, (turn + 2) * each, start_block, 0)
+        for j in range(each):
+            start_block(turn * each + (j + 1))
         add_blocks(turn * CHUNK, CHUNK)
         return carry
 
@@ -362,26 +392,15 @@
         b2 = jnp.where(lane < 2, roll(pv, 2), roll(v, 2))
         sm = (6.0 * v + 4.0 * (a1 + b1) + (a2 + b2)) * 0.0625
         for k in range(2):
-            smooth_ref[c, pl.ds(k, n, stride=2), :] = sm[k * n : (k + 1) * n]
+            held_ref[c, pl.ds(k, n, stride=2), :] = sm[k * n : (k + 1) * n]
         after = (
             6.0 * roll(nx, -1) + 4.0 * (roll(nx, -2) + v) + (roll(nx, -3) + roll(v, 1))
         ) * 0.0625
         ahead = jnp.where(lane < LANES - 1, roll(sm, -1), after)
         arrays += [0.5 * (ahead + sm), ahead - sm]
-    pick = jnp.zeros((8, LANES), F32)
-    for j, where in enumerate(EDGE_LANES):
-        hit = jnp.logical_and(iota((8, LANES), 0) == j, iota((8, LANES), 1) == where)
-        pick = pick + jnp.where(hit, 1.0, 0.0)
-    stack = jnp.concatenate([part for array in arrays for part in three_parts(array)], axis=0)
-    got = lax.dot_general(
-        pick.astype(BF16), stack, (((1,), (1,)), ((), ())), preferred_element_type=F32
-    )
-    got = [
-        got[:, 3 * m * held : (3 * m + 1) * held]
-        + got[:, (3 * m + 1) * held : (3 * m + 2) * held]
-        + got[:, (3 * m + 2) * held : (3 * m + 3) * held]
-        for m in range(6)
-    ]
+    got = pick_lanes(EDGE_LANES, arrays)
+    written = pltpu.make_async_copy(held_ref, smooth_ref, out_sem)
+    written.start()
     rows, highs, lows = features(got[0::2], got[1::2])
     for k in range(2):
         at = slice(k * n, (k + 1) * n)
@@ -397,11 +416,20 @@
         at = slice(h * half, (h + 1) * half)
         t = [tgt_ref[h * 3 + c : h * 3 + c + 1, :] for c in range(3)]
         s = [acc_ref[k : k + 1, at] + acc_ref[8 + k : 9 + k, at] for k in range(6)]
-        sum_ref[0:1, at] = scale * (s[1] * t[2] - s[2] * t[1] - s[3])
-        sum_ref[1:2, at] = scale * (s[2] * t[0] - s[0] * t[2] - s[4])
-        sum_ref[2:3, at] = scale * (s[0] * t[1] - s[1] * t[0] - s[5])
-    copies = send_row(lambda to: piece(sum_ref, to, panel), lambda r: row_sum.at[r], s4, r4)
-    row_sum[me_r] = sum_ref[:, pl.ds(pl.multiple_of(me_r * panel, panel), panel)]
+        v = [
+            scale * (s[1] * t[2] - s[2] * t[1] - s[3]),
+            scale * (s[2] * t[0] - s[0] * t[2] - s[4]),
+            scale * (s[0] * t[1] - s[1] * t[0] - s[5]),
+        ]
+        for m in range(half // LANES):
+            group = (h * half + m * LANES) // panel
+            for c in range(3):
+                row = 2 * c + m % 2
+                sum_ref[row : row + 1, group * LANES : (group + 1) * LANES] = v[c][
+                    :, m * LANES : (m + 1) * LANES
+                ]
+    copies = send_row(lambda to: piece(sum_ref, to, LANES), lambda r: row_sum.at[r], s4, r4)
+    row_sum[me_r] = sum_ref[:, pl.ds(pl.multiple_of(me_r * LANES, LANES), LANES)]
     wait_from(me_r, n_row, lambda r: row_sum.at[r], r4)
     value = add_up(row_sum, n_row)
     row_total[...] = value
@@ -409,12 +437,18 @@
     col_sum[me_c] = value
     wait_from(me_c, n_col, lambda c: col_sum.at[c], r5)
     value = add_up(col_sum, n_col)
-    share = vel_ref.shape[1]
-    pick = (iota((panel, share), 0) == me_c * share + iota((panel, share), 1)).astype(BF16)
+    share = vel_ref.shape[2]
+    per_row = LANES // share
+    first = lax.rem(me_c, per_row) * share
+    pick = (iota((LANES, share), 0) == first + iota((LANES, share), 1)).astype(BF16)
     got = [jnp.dot(part, pick, preferred_element_type=F32) for part in three_parts(value)]
-    vel_ref[...] = (got[0] + got[1] + got[2])[:3]
+    got = got[0] + got[1] + got[2]
+    lower = (iota((1, share), 1) + me_c) < iota((1, share), 1) + per_row
+    for c in range(3):
+        vel_ref[c] = jnp.where(lower, got[2 * c : 2 * c + 1], got[2 * c + 1 : 2 * c + 2])
     for copy in copies:
         copy.wait_send()
+    written.wait()
 
 
 def shards(n_row, n_col, positions, block_links, panel_points):
@@ -433,10 +467,10 @@
         functools.partial(step_kernel, n_row, n_col, scale),
         out_shape=(
             jax.ShapeDtypeStruct((3, held, block_len), F32),
-            jax.ShapeDtypeStruct((3, panel // n_col), F32),
+            jax.ShapeDtypeStruct((3, 1, panel // n_col), F32),
         ),
         in_specs=[whole, whole, whole],
-        out_specs=(whole, whole),
+        out_specs=(pl.BlockSpec(memory_space=pl.ANY), whole),
         scratch_shapes=[
             pltpu.VMEM((2, devices, slots), F32),
             pltpu.VMEM((8, targets // 2), F32),
@@ -448,14 +482,15 @@
             pltpu.VMEM((32, targets), F32),
             pltpu.VMEM((16, targets), F32),
             pltpu.VMEM((2, held, held), F32),
-            pltpu.VMEM((8, targets), F32),
+            pltpu.VMEM((8, groups * LANES), F32),
             pltpu.VMEM((n_row, 8, width), F32),
             pltpu.VMEM((8, width), F32),
             pltpu.VMEM((n_col, 8, width), F32),
-            pltpu.VMEM((n_row, 8, panel), F32),
-            pltpu.VMEM((8, panel), F32),
-            pltpu.VMEM((n_col, 8, panel), F32),
-            dma, dma,
+            pltpu.VMEM((n_row, 8, LANES), F32),
+            pltpu.VMEM((8, LANES), F32),
+            pltpu.VMEM((n_col, 8, LANES), F32),
+            pltpu.VMEM((3, held, block_len), F32),
+            dma, dma, dma,
             dma((n_row,)), dma((n_row,)),
             dma((n_col,)), dma((n_col,)),
             dma((n_row,)), dma((n_row,)),
@@ -467,7 +502,7 @@
         ),
         name="step",
     )(positions, block_links, panel_points)
-    return smoothed, velocity[None]
+    return smoothed, jnp.transpose(velocity, (1, 0, 2))
 
 
 def solution(mesh):

time: 89.2 us -> 81.5 us (0.914)
  Pallas kernels: 85.3 us -> 78.3 us
    pallas_call x1, Pallas kernels: 85.3 us -> 78.3 us  [shards(): pl.pallas_call(functools.partial(step_kernel, n_row, n_col, scale), out_s...]
where the time goes in v3:
time: 81.5 us; the launch traced here: 81.3 us
  Pallas kernels  78.3 us (96%)
  local copies, waits for them, and re-layouts  2.33 us (3%)
    pallas_call x1, Pallas kernels, shards(): pl.pallas_call(functools.partial(step_kernel, n_row, n_col, scale), out_s...  78.3 us
    unnamed x4, local copies, waits for them, and re-layouts  2.33 us

profile of v3, /device:TPU:1, one launch (start us, length us, event | category | flops | bytes accessed | tf_op | source)
XLA Modules:
  0.0 81.3 jit_solution(8681066666437403170)
XLA Ops:
  0.6 78.3 %step.1 = (f32[3,256,128]{2,1,0:T(8,128)}, f32[3,1,16]{2,1,0:T(1,128)}) custom-call(f32[3,128,128]{2,1,0:T(8,128)} %pos_ref.1, s32[2,16384]{1,0:T(2,128)} %links_ref.1, s32[8,256]{1,0:T(8,128)} %panel_ref.1), custom_call_target="tpu_custom_call" | custom-call | tf_op jit(solution)/shard_map/step/pallas_call | solution.py:466
  79.0 0.0 copy-start
  79.0 1.8 %copy.7 = f32[3,256,128]{2,1,0:T(8,128)} copy(f32[3,256,128]{2,1,0:T(8,128)} %get-tuple-element.8) | data formatting | bytes 786432
  80.8 0.0 copy-done
  80.8 0.6 copy.8
Async XLA Ops:
  79.0 1.8 %copy-start = (f32[3,1,16]{2,1,0:T(1,128)S(1)}, f32[3,1,16]{2,1,0:T(1,128)}, u32[]{:S(2)}) copy-start(f32[3,1,16]{2,1,0:T(1,128)} %get-tuple-element.5) | copy-start | bytes 580

commit v4 on v3

--- a/solution.py
+++ b/solution.py
@@ -15,7 +15,6 @@
 VMEM_LIMIT = 56 << 20
 MESH = pl.DeviceIdType.MESH
 CHUNK = 32
-TILE = 256
 EDGE_LANES = (125, 126, 127, 0, 1)
 
 
@@ -202,8 +201,6 @@
     edges = pick_lanes((LANES - 2, LANES - 1, 0, 1), wraps)
     edge_parts = jnp.concatenate([part for edge in edges for part in three_parts(edge)], axis=0)
     panel = panel_ref.shape[1]
-    half = tgt_ref.shape[1]
-    per_half = half // panel
     part_ref[...] = jnp.zeros_like(part_ref)
     kind = iota((8, panel), 0)
     edge_point = jnp.where(kind < 2, kind + (LANES - 2), jnp.where(kind < 4, kind - 2, -1))
@@ -229,14 +226,18 @@
             value = jnp.sum(inner, axis=0, keepdims=True) + jnp.sum(
                 jnp.where(edge_point == point, outer, 0.0), axis=0, keepdims=True
             )
-            row = (r // per_half) * 3 + c
-            col = (r % per_half) * panel
-            part_ref[row : row + 1, col : col + panel] = value
-
-    width = half // n_row
+            for h in range(2):
+                part_ref[2 * c + h : 2 * c + h + 1, r * LANES : (r + 1) * LANES] = value[
+                    :, h * LANES : (h + 1) * LANES
+                ]
+
+    width = LANES
+
+    def lanes(r, size):
+        return pl.ds(pl.multiple_of(r * size, size), size)
 
     def piece(ref, r, size):
-        return ref.at[:, pl.ds(pl.multiple_of(r * size, size), size)]
+        return ref.at[:, lanes(r, size)]
 
     pl.semaphore_wait(barrier, n_row + n_col - 2)
     copies = send_row(lambda to: piece(part_ref, to, width), lambda r: row_in.at[r], s1, r1)
@@ -302,27 +303,23 @@
             pair_ref[0, at[0], at[1]] = jnp.where(nexts[k] == id_rows[m], 1.0, 0.0)
             pair_ref[1, at[0], at[1]] = jnp.where(ids[k] == next_rows[m], 1.0, 0.0)
 
-    wait_from(me_r, n_row, lambda r: piece(tgt_ref, r, width), r3)
-    for copy in copies:
-        copy.wait_send()
-
-    a_ref[...] = jnp.zeros_like(a_ref)
-    for h in range(2):
-        at = slice(h * half, (h + 1) * half)
-        t = [tgt_ref[h * 3 + c : h * 3 + c + 1, :] for c in range(3)]
-        rows = []
-        for value in t:
-            top, middle, low = (part.astype(F32) for part in three_parts(-2.0 * value))
-            rows += [top, top, middle, top, low, middle]
-        rows += [jnp.ones_like(t[0])] * 3
-        square = t[0] * t[0] + t[1] * t[1] + t[2] * t[2] + CORE_SQUARED
-        rows += [part.astype(F32) for part in three_parts(square)]
-        for k, row in enumerate(rows):
-            a_ref[k : k + 1, at] = row
-
-    acc_ref[...] = jnp.zeros_like(acc_ref)
-
-    def add_blocks(first, count):
+    def aim(r):
+        value = tgt_ref[:, lanes(r, LANES)]
+        top, middle, low = (part.astype(F32) for part in three_parts(-2.0 * value))
+        square = value * value
+        for h in range(2):
+            at = pl.ds(pl.multiple_of(r * panel + h * LANES, LANES), LANES)
+            k = 0
+            for c in range(3):
+                for part in (top, top, middle, top, low, middle):
+                    a_ref[k : k + 1, at] = part[2 * c + h : 2 * c + h + 1]
+                    k += 1
+            a_ref[k : k + 3, at] = jnp.ones((3, LANES), F32)
+            total_square = square[h : h + 1] + square[2 + h : 3 + h] + square[4 + h : 5 + h]
+            for m, part in enumerate(three_parts(total_square + CORE_SQUARED)):
+                a_ref[k + 3 + m : k + 4 + m, at] = part.astype(F32)
+
+    def add_blocks(first, count, panels):
         b_at = pl.multiple_of(first * 32, 32)
         f_at = pl.multiple_of(first * 16, 16)
         b = jnp.concatenate(
@@ -331,14 +328,42 @@
         f = jnp.concatenate(
             [f_ref[pl.ds(f_at + 16 * j, 16), :].astype(BF16) for j in range(count)], axis=1
         )
-        for at in range(0, acc_ref.shape[1], TILE):
-            a = a_ref[:, at : at + TILE].astype(BF16)
+        for r in panels:
+            at = lanes(r, panel)
+            a = a_ref[:, at].astype(BF16)
             q = lax.dot_general(b, a, (((0,), (0,)), ((), ())), preferred_element_type=F32)
-            r = lax.rsqrt(q)
-            top, low = two_parts(r * r * r)
-            acc_ref[:, at : at + TILE] += jnp.dot(f, top, preferred_element_type=F32) + jnp.dot(
+            root = lax.rsqrt(q)
+            top, low = two_parts(root * root * root)
+            acc_ref[:, at] += jnp.dot(f, top, preferred_element_type=F32) + jnp.dot(
                 f, low, preferred_element_type=F32
             )
+
+    def velocity_of(r):
+        value = tgt_ref[:, lanes(r, LANES)]
+        for h in range(2):
+            at = pl.ds(pl.multiple_of(r * panel + h * LANES, LANES), LANES)
+            t = [value[2 * c + h : 2 * c + h + 1] for c in range(3)]
+            s = [acc_ref[k : k + 1, at] + acc_ref[8 + k : 9 + k, at] for k in range(6)]
+            v = [
+                scale * (s[1] * t[2] - s[2] * t[1] - s[3]),
+                scale * (s[2] * t[0] - s[0] * t[2] - s[4]),
+                scale * (s[0] * t[1] - s[1] * t[0] - s[5]),
+            ]
+            for c in range(3):
+                sum_ref[2 * c + h : 2 * c + h + 1, lanes(r, LANES)] = v[c]
+
+    others = [lax.rem(me_r + k, n_row) for k in range(1, n_row)]
+    acc_ref[...] = jnp.zeros_like(acc_ref)
+    sum_ref[...] = jnp.zeros_like(sum_ref)
+    a_ref[...] = jnp.zeros_like(a_ref)
+    aim(me_r)
+    for first in range(0, slots // 2, CHUNK // 2):
+        add_blocks(first, CHUNK // 2, [me_r])
+    wait_from(me_r, n_row, lambda r: piece(tgt_ref, r, width), r3)
+    for copy in copies:
+        copy.wait_send()
+    for r in others:
+        aim(r)
 
     def tile(ref, device):
         return ref.at[pl.ds(pl.multiple_of(device * 8, 8), 8), :]
@@ -355,20 +380,19 @@
         ).start()
 
     turns = slots // CHUNK
-    each = (n - 1) // (turns - 1)
+    each = (n - 1) // turns
     own = pl.ds(pl.multiple_of(me * 8, 8), 8)
     arrived_ref[own, :] = send_ref[own, :]
-    for step in range(each * (turns - 1) + 1, n):
+    for step in range(each * turns + 1, n):
         start_block(step)
 
     def chunk(turn, carry):
         for j in range(each):
             start_block(turn * each + (j + 1))
-        add_blocks(turn * CHUNK, CHUNK)
+        add_blocks(turn * CHUNK, CHUNK, others)
         return carry
 
-    lax.fori_loop(0, turns - 1, chunk, 0)
-    add_blocks((turns - 1) * CHUNK, CHUNK)
+    lax.fori_loop(0, turns, chunk, 0)
 
     rest = pl.ds(0, 8 * (n - 1))
     pltpu.make_async_copy(arrived_ref.at[rest], arrived_ref.at[rest], recv_sem).wait()
@@ -409,26 +433,15 @@
         for m in range(6):
             f_ref[pl.ds((slots + k) * 16 + m, 8, stride=32), :] = highs[m][:, at]
             f_ref[pl.ds((slots + k) * 16 + 8 + m, 8, stride=32), :] = lows[m][:, at]
-    add_blocks(slots, 2 * len(EDGE_LANES))
-
-    sum_ref[...] = jnp.zeros_like(sum_ref)
-    for h in range(2):
-        at = slice(h * half, (h + 1) * half)
-        t = [tgt_ref[h * 3 + c : h * 3 + c + 1, :] for c in range(3)]
-        s = [acc_ref[k : k + 1, at] + acc_ref[8 + k : 9 + k, at] for k in range(6)]
-        v = [
-            scale * (s[1] * t[2] - s[2] * t[1] - s[3]),
-            scale * (s[2] * t[0] - s[0] * t[2] - s[4]),
-            scale * (s[0] * t[1] - s[1] * t[0] - s[5]),
-        ]
-        for m in range(half // LANES):
-            group = (h * half + m * LANES) // panel
-            for c in range(3):
-                row = 2 * c + m % 2
-                sum_ref[row : row + 1, group * LANES : (group + 1) * LANES] = v[c][
-                    :, m * LANES : (m + 1) * LANES
-                ]
+    add_blocks(slots, 2 * len(EDGE_LANES), others)
+
+    for r in others:
+        velocity_of(r)
     copies = send_row(lambda to: piece(sum_ref, to, LANES), lambda r: row_sum.at[r], s4, r4)
+    for first in range(slots // 2, slots, CHUNK // 2):
+        add_blocks(first, CHUNK // 2, [me_r])
+    add_blocks(slots, 2 * len(EDGE_LANES), [me_r])
+    velocity_of(me_r)
     row_sum[me_r] = sum_ref[:, pl.ds(pl.multiple_of(me_r * LANES, LANES), LANES)]
     wait_from(me_r, n_row, lambda r: row_sum.at[r], r4)
     value = add_up(row_sum, n_row)
@@ -458,7 +471,7 @@
     blocks = block_links.shape[1]
     groups, panel = panel_points.shape
     targets = groups * panel
-    width = targets // 2 // n_row
+    width = LANES
     stored = slots + 2 * 8
     scale = 1.0 / (math.pi * math.sqrt(blocks * block_len))
     whole = pl.BlockSpec(memory_space=pltpu.VMEM)
@@ -473,8 +486,8 @@
         out_specs=(pl.BlockSpec(memory_space=pl.ANY), whole),
         scratch_shapes=[
             pltpu.VMEM((2, devices, slots), F32),
-            pltpu.VMEM((8, targets // 2), F32),
-            pltpu.VMEM((8, targets // 2), F32),
+            pltpu.VMEM((8, groups * LANES), F32),
+            pltpu.VMEM((8, groups * LANES), F32),
             pltpu.VMEM((8 * devices, block_len), F32),
             pltpu.VMEM((8 * devices, block_len), F32),
             pltpu.VMEM((stored * 32, LANES), F32),

time: 81.5 us -> 76.8 us (0.942)
  Pallas kernels: 78.3 us -> 73.7 us
    pallas_call x1, Pallas kernels: 78.3 us -> 73.7 us  [shards(): pl.pallas_call(functools.partial(step_kernel, n_row, n_col, scale), out_s...]
where the time goes in v4:
time: 76.8 us; the launch traced here: 76.6 us
  Pallas kernels  73.7 us (96%)
  local copies, waits for them, and re-layouts  2.33 us (3%)
    pallas_call x1, Pallas kernels, shards(): pl.pallas_call(functools.partial(step_kernel, n_row, n_col, scale), out_s...  73.7 us
    unnamed x4, local copies, waits for them, and re-layouts  2.33 us

profile of v4, /device:TPU:1, one launch (start us, length us, event | category | flops | bytes accessed | tf_op | source)
XLA Modules:
  0.0 76.6 jit_solution(2678616153187535307)
XLA Ops:
  0.6 73.7 %step.1 = (f32[3,256,128]{2,1,0:T(8,128)}, f32[3,1,16]{2,1,0:T(1,128)}) custom-call(f32[3,128,128]{2,1,0:T(8,128)} %pos_ref.1, s32[2,16384]{1,0:T(2,128)} %links_ref.1, s32[8,256]{1,0:T(8,128)} %panel_ref.1), custom_call_target="tpu_custom_call" | custom-call | tf_op jit(solution)/shard_map/step/pallas_call | solution.py:479
  74.3 0.0 copy-start
  74.3 1.8 %copy.7 = f32[3,256,128]{2,1,0:T(8,128)} copy(f32[3,256,128]{2,1,0:T(8,128)} %get-tuple-element.8) | data formatting | bytes 786432
  76.1 0.0 copy-done
  76.1 0.6 copy.8
Async XLA Ops:
  74.3 1.8 %copy-start = (f32[3,1,16]{2,1,0:T(1,128)S(1)}, f32[3,1,16]{2,1,0:T(1,128)}, u32[]{:S(2)}) copy-start(f32[3,1,16]{2,1,0:T(1,128)} %get-tuple-element.5) | copy-start | bytes 580

commit v5 on v4

--- a/solution.py
+++ b/solution.py
@@ -106,6 +106,14 @@
     n = n_row * n_col
     slots = pos_ref.shape[1]
     held = 2 * n
+    moves = [(y, z, k) for y in range(n_col // 4) for z in range(2) for k in range(2)][1:]
+    moves.sort(key=lambda m: -(min(m[0], n_col // 4 - m[0]) + 2 * m[1]))
+    far_first = [
+        4 * lax.rem(me_c // 4 + y, n_col // 4)
+        + 2 * lax.rem(me_c // 2 + z, 2)
+        + lax.rem(me_c + k, 2)
+        for y, z, k in moves
+    ]
 
     barrier = pltpu.get_barrier_semaphore()
     for step in range(1, n_row):
@@ -115,9 +123,9 @@
         to = lax.rem(me_c + step, n_col)
         pl.semaphore_signal(barrier, inc=1, device_id=(me_r, to), device_id_type=MESH)
 
-    def send_row(source, target, send, recv):
+    def send_row(source, target, send, recv, steps=tuple(range(1, n_row))):
         copies = []
-        for step in range(1, n_row):
+        for step in steps:
             to = lax.rem(me_r + step, n_row)
             copy = pltpu.make_async_remote_copy(
                 src_ref=source(to),
@@ -133,8 +141,7 @@
 
     def send_col(source, target, send, recv):
         copies = []
-        for step in range(1, n_col):
-            to = lax.rem(me_c + step, n_col)
+        for step, to in enumerate(far_first):
             copy = pltpu.make_async_remote_copy(
                 src_ref=source,
                 dst_ref=target(me_c),
@@ -147,8 +154,8 @@
             copies.append(copy)
         return copies
 
-    def wait_from(mine, count, target, recv):
-        for step in range(1, count):
+    def wait_from(mine, count, target, recv, steps=None):
+        for step in steps or range(1, count):
             frm = lax.rem(mine + step, count)
             pltpu.make_async_copy(target(frm), target(frm), recv.at[frm]).wait()
 
@@ -352,14 +359,21 @@
             for c in range(3):
                 sum_ref[2 * c + h : 2 * c + h + 1, lanes(r, LANES)] = v[c]
 
-    others = [lax.rem(me_r + k, n_row) for k in range(1, n_row)]
+    near = n_row // 2
+    far = [k for k in range(1, n_row) if k != near]
+    others = [lax.rem(me_r + k, n_row) for k in far]
+    near_r = lax.rem(me_r + near, n_row)
     acc_ref[...] = jnp.zeros_like(acc_ref)
     sum_ref[...] = jnp.zeros_like(sum_ref)
     a_ref[...] = jnp.zeros_like(a_ref)
     aim(me_r)
     for first in range(0, slots // 2, CHUNK // 2):
         add_blocks(first, CHUNK // 2, [me_r])
-    wait_from(me_r, n_row, lambda r: piece(tgt_ref, r, width), r3)
+    wait_from(me_r, n_row, lambda r: piece(tgt_ref, r, width), r3, [near])
+    aim(near_r)
+    for first in range(0, slots // 2, CHUNK // 2):
+        add_blocks(first, CHUNK // 2, [near_r])
+    wait_from(me_r, n_row, lambda r: piece(tgt_ref, r, width), r3, far)
     for copy in copies:
         copy.wait_send()
     for r in others:
@@ -437,7 +451,13 @@
 
     for r in others:
         velocity_of(r)
-    copies = send_row(lambda to: piece(sum_ref, to, LANES), lambda r: row_sum.at[r], s4, r4)
+    for_row = (lambda to: piece(sum_ref, to, LANES), lambda r: row_sum.at[r], s4, r4)
+    copies = send_row(*for_row, far)
+    for first in range(slots // 2, slots, CHUNK // 2):
+        add_blocks(first, CHUNK // 2, [near_r])
+    add_blocks(slots, 2 * len(EDGE_LANES), [near_r])
+    velocity_of(near_r)
+    copies += send_row(*for_row, [near])
     for first in range(slots // 2, slots, CHUNK // 2):
         add_blocks(first, CHUNK // 2, [me_r])
     add_blocks(slots, 2 * len(EDGE_LANES), [me_r])

time: 76.8 us -> 75.9 us (0.988)
  Pallas kernels: 73.7 us -> 72.7 us
    pallas_call x1, Pallas kernels: 73.7 us -> 72.7 us  [shards(): pl.pallas_call(functools.partial(step_kernel, n_row, n_col, scale), out_s...]
where the time goes in v5:
time: 75.9 us; the launch traced here: 75.7 us
  Pallas kernels  72.7 us (96%)
  local copies, waits for them, and re-layouts  2.33 us (3%)
    pallas_call x1, Pallas kernels, shards(): pl.pallas_call(functools.partial(step_kernel, n_row, n_col, scale), out_s...  72.7 us
    unnamed x4, local copies, waits for them, and re-layouts  2.33 us

profile of v5, /device:TPU:1, one launch (start us, length us, event | category | flops | bytes accessed | tf_op | source)
XLA Modules:
  0.0 75.7 jit_solution(13303311313915089421)
XLA Ops:
  0.6 72.7 %step.1 = (f32[3,256,128]{2,1,0:T(8,128)}, f32[3,1,16]{2,1,0:T(1,128)}) custom-call(f32[3,128,128]{2,1,0:T(8,128)} %pos_ref.1, s32[2,16384]{1,0:T(2,128)} %links_ref.1, s32[8,256]{1,0:T(8,128)} %panel_ref.1), custom_call_target="tpu_custom_call" | custom-call | tf_op jit(solution)/shard_map/step/pallas_call | solution.py:499
  73.4 0.0 copy-start
  73.4 1.8 %copy.7 = f32[3,256,128]{2,1,0:T(8,128)} copy(f32[3,256,128]{2,1,0:T(8,128)} %get-tuple-element.8) | data formatting | bytes 786432
  75.1 0.0 copy-done
  75.1 0.6 copy.8
Async XLA Ops:
  73.4 1.8 %copy-start = (f32[3,1,16]{2,1,0:T(1,128)S(1)}, f32[3,1,16]{2,1,0:T(1,128)}, u32[]{:S(2)}) copy-start(f32[3,1,16]{2,1,0:T(1,128)} %get-tuple-element.5) | copy-start | bytes 580

commit v6 on v5

--- a/solution.py
+++ b/solution.py
@@ -15,6 +15,8 @@
 VMEM_LIMIT = 56 << 20
 MESH = pl.DeviceIdType.MESH
 CHUNK = 32
+PART = 8
+SMALL = 8
 EDGE_LANES = (125, 126, 127, 0, 1)
 
 
@@ -367,12 +369,12 @@
     sum_ref[...] = jnp.zeros_like(sum_ref)
     a_ref[...] = jnp.zeros_like(a_ref)
     aim(me_r)
-    for first in range(0, slots // 2, CHUNK // 2):
-        add_blocks(first, CHUNK // 2, [me_r])
+    for first in range(0, slots // 2, SMALL):
+        add_blocks(first, SMALL, [me_r])
     wait_from(me_r, n_row, lambda r: piece(tgt_ref, r, width), r3, [near])
     aim(near_r)
-    for first in range(0, slots // 2, CHUNK // 2):
-        add_blocks(first, CHUNK // 2, [near_r])
+    for first in range(0, slots // 2, SMALL):
+        add_blocks(first, SMALL, [near_r])
     wait_from(me_r, n_row, lambda r: piece(tgt_ref, r, width), r3, far)
     for copy in copies:
         copy.wait_send()
@@ -403,7 +405,8 @@
     def chunk(turn, carry):
         for j in range(each):
             start_block(turn * each + (j + 1))
-        add_blocks(turn * CHUNK, CHUNK, others)
+        for first in range(0, CHUNK, PART):
+            add_blocks(turn * CHUNK + first, PART, others)
         return carry
 
     lax.fori_loop(0, turns, chunk, 0)
@@ -453,13 +456,13 @@
         velocity_of(r)
     for_row = (lambda to: piece(sum_ref, to, LANES), lambda r: row_sum.at[r], s4, r4)
     copies = send_row(*for_row, far)
-    for first in range(slots // 2, slots, CHUNK // 2):
-        add_blocks(first, CHUNK // 2, [near_r])
+    for first in range(slots // 2, slots, SMALL):
+        add_blocks(first, SMALL, [near_r])
     add_blocks(slots, 2 * len(EDGE_LANES), [near_r])
     velocity_of(near_r)
     copies += send_row(*for_row, [near])
-    for first in range(slots // 2, slots, CHUNK // 2):
-        add_blocks(first, CHUNK // 2, [me_r])
+    for first in range(slots // 2, slots, SMALL):
+        add_blocks(first, SMALL, [me_r])
     add_blocks(slots, 2 * len(EDGE_LANES), [me_r])
     velocity_of(me_r)
     row_sum[me_r] = sum_ref[:, pl.ds(pl.multiple_of(me_r * LANES, LANES), LANES)]

time: 75.9 us -> 73.9 us (0.974)
  Pallas kernels: 72.7 us -> 70.8 us
    pallas_call x1, Pallas kernels: 72.7 us -> 70.8 us  [shards(): pl.pallas_call(functools.partial(step_kernel, n_row, n_col, scale), out_s...]
where the time goes in v6:
time: 73.9 us; the launch traced here: 73.8 us
  Pallas kernels  70.8 us (96%)
  local copies, waits for them, and re-layouts  2.33 us (3%)
    pallas_call x1, Pallas kernels, shards(): pl.pallas_call(functools.partial(step_kernel, n_row, n_col, scale), out_s...  70.8 us
    unnamed x4, local copies, waits for them, and re-layouts  2.33 us

profile of v6, /device:TPU:1, one launch (start us, length us, event | category | flops | bytes accessed | tf_op | source)
XLA Modules:
  0.0 73.8 jit_solution(10739872470687784724)
XLA Ops:
  0.6 70.8 %step.1 = (f32[3,256,128]{2,1,0:T(8,128)}, f32[3,1,16]{2,1,0:T(1,128)}) custom-call(f32[3,128,128]{2,1,0:T(8,128)} %pos_ref.1, s32[2,16384]{1,0:T(2,128)} %links_ref.1, s32[8,256]{1,0:T(8,128)} %panel_ref.1), custom_call_target="tpu_custom_call" | custom-call | tf_op jit(solution)/shard_map/step/pallas_call | solution.py:502
  71.4 0.0 copy-start
  71.4 1.8 %copy.7 = f32[3,256,128]{2,1,0:T(8,128)} copy(f32[3,256,128]{2,1,0:T(8,128)} %get-tuple-element.8) | data formatting | bytes 786432
  73.2 0.0 copy-done
  73.2 0.6 copy.8
Async XLA Ops:
  71.4 1.8 %copy-start = (f32[3,1,16]{2,1,0:T(1,128)S(1)}, f32[3,1,16]{2,1,0:T(1,128)}, u32[]{:S(2)}) copy-start(f32[3,1,16]{2,1,0:T(1,128)} %get-tuple-element.5) | copy-start | bytes 580

commit v7 on v6

--- a/solution.py
+++ b/solution.py
@@ -15,7 +15,7 @@
 VMEM_LIMIT = 56 << 20
 MESH = pl.DeviceIdType.MESH
 CHUNK = 32
-PART = 8
+PART = 4
 SMALL = 8
 EDGE_LANES = (125, 126, 127, 0, 1)
 

time: 73.9 us -> 73.7 us (level)
  no operation moved by 1% of the time
where the time goes in v7:
time: 73.7 us; the launch traced here: 73.6 us
  Pallas kernels  70.6 us (96%)
  local copies, waits for them, and re-layouts  2.33 us (3%)
    pallas_call x1, Pallas kernels, shards(): pl.pallas_call(functools.partial(step_kernel, n_row, n_col, scale), out_s...  70.6 us
    unnamed x4, local copies, waits for them, and re-layouts  2.33 us

profile of v7, /device:TPU:1, one launch (start us, length us, event | category | flops | bytes accessed | tf_op | source)
XLA Modules:
  0.0 73.6 jit_solution(6115371608329122508)
XLA Ops:
  0.6 70.6 %step.1 = (f32[3,256,128]{2,1,0:T(8,128)}, f32[3,1,16]{2,1,0:T(1,128)}) custom-call(f32[3,128,128]{2,1,0:T(8,128)} %pos_ref.1, s32[2,16384]{1,0:T(2,128)} %links_ref.1, s32[8,256]{1,0:T(8,128)} %panel_ref.1), custom_call_target="tpu_custom_call" | custom-call | tf_op jit(solution)/shard_map/step/pallas_call | solution.py:502
  71.2 0.0 copy-start
  71.2 1.8 %copy.7 = f32[3,256,128]{2,1,0:T(8,128)} copy(f32[3,256,128]{2,1,0:T(8,128)} %get-tuple-element.8) | data formatting | bytes 786432
  73.0 0.0 copy-done
  73.0 0.6 copy.8
Async XLA Ops:
  71.2 1.8 %copy-start = (f32[3,1,16]{2,1,0:T(1,128)S(1)}, f32[3,1,16]{2,1,0:T(1,128)}, u32[]{:S(2)}) copy-start(f32[3,1,16]{2,1,0:T(1,128)} %get-tuple-element.5) | copy-start | bytes 580
